TPU v7x, 128 devices: a whole 4x4x4 slice. The times are simulated.
128 devices in a mesh: dev: 128 (over x, z, y, core).
Axes of the slice: x: 4, y: 4, z: 4, core: 2. Of those that a mesh axis runs over, the one named last changes fastest.
Arguments:
- node_coords: float32 [3, 65536], P(None, 'dev'), may hold values from 0 to 1
- node_disp: float32 [3, 65536], P(None, 'dev'), may hold values from -6 to 6
- node_list: int32 [128, 1024], P('dev'), may hold values from 0 to 65535, as said below
- factor: float32 [128, 1024, 1024], P('dev'), may hold values from -1 to 2, as said below
- fluid_coords: float32 [3, 524288], P(None, 'dev'), may hold values from 0 to 1
- fluid_loads: float32 [3, 524288], P(None, 'dev'), may hold values from -6 to 6
- fluid_patch: int32 [524288, 4], P('dev'), may hold values from 0 to 127, all different within a row; in each aligned block of 4096 rows (0 to 4095, 4096 to 8191, ...) at most 256 rows name the same one
- blend_raw: float32 [524288, 4], P('dev'), may hold values from 0.1 to 1
Outputs:
- fluid_disp: float32 [3, 524288], P(None, 'dev')
- node_loads: float32 [3, 65536], P(None, 'dev')
Inputs may be any that keep to these rules, and one draw needn't show every extreme that they name: `node_list`: the 1024 entries of one patch name nodes of exactly 64 distinct devices (node n belongs to device n // 512), exactly 16 entries for each of them; a node may appear more than once. factor[p] is lower triangular with diagonal entries between 1 and 2. `fluid_patch`: in each aligned block of 4096 points no patch is named by more than 256 points.
All inputs are finite; a program needn't handle non-finite values.
Results may differ from a plain program's by a relative error of at most 0.0003.
Values sent between devices are 32-bit elements; how exact they have to be, the bound alone decides.
A program may use at most 192 MiB of HBM per device.

v0:
```python
import math

import jax
import jax.numpy as jnp
from jax import lax
from jax.sharding import PartitionSpec as P

PN = 1024
SLOTS = 4


kernel_gain = 8.0
highest = lax.Precision.HIGHEST


def kernel_tile(points, centres):
    squared = jnp.zeros((points.shape[1], centres.shape[1]), jnp.float32)
    for component in range(3):
        offset = points[component][:, None] - centres[component][None, :]
        squared = squared + offset * offset
    return lax.rsqrt(1.0 + kernel_gain * squared) / math.sqrt(PN)


def apply_inverse(values, inverse):
    partial_value = lax.dot_general(values, inverse, (((1,), (1,)), ((), ())), precision=highest)
    return jnp.dot(partial_value, inverse, precision=highest)


def rank_in_block(targets, classes):
    onehot = (targets[:, None] == jnp.arange(classes, dtype=jnp.int32)[None, :]).astype(jnp.int32)
    before = jnp.cumsum(onehot, axis=0) - onehot
    return jnp.sum(before * onehot, axis=1)


def local(
    node_coords, node_disp, node_list, factor, fluid_coords, fluid_loads, fluid_patch, blend_raw
):
    devices = lax.axis_size("dev")
    node_ids = node_list[0]
    inverse = factor[0]
    node_count = node_disp.shape[1]
    local_table = jnp.concatenate([node_coords, node_disp], axis=0)
    whole_table = lax.all_gather(local_table, "dev", axis=1, tiled=True)
    gathered = jnp.take(whole_table, node_ids, axis=1)
    centres = gathered[:3]
    coeffs = apply_inverse(gathered[3:], inverse)
    blends = blend_raw / jnp.sum(blend_raw, axis=1, keepdims=True)
    weight_flat = blends.reshape(-1)
    targets = fluid_patch.reshape(-1)
    entry_count = targets.shape[0]
    bucket = 2 * entry_count // devices
    point_slot = targets * bucket + rank_in_block(targets, devices)
    point_row = jnp.arange(entry_count, dtype=jnp.int32) // SLOTS
    payload = jnp.concatenate(
        [fluid_coords[:, point_row], weight_flat[None, :] * fluid_loads[:, point_row]], axis=0
    )
    send_points = jnp.zeros((6, devices * bucket), jnp.float32).at[:, point_slot].set(payload)
    received = lax.all_to_all(send_points, "dev", split_axis=1, concat_axis=1, tiled=True)
    total_rows = devices * bucket
    block_rows = math.gcd(total_rows, 2048)
    blocks = jnp.transpose(received.reshape(6, total_rows // block_rows, block_rows), (1, 0, 2))

    def tile_step(accumulated, block_data):
        tile_vals = kernel_tile(block_data[:3], centres)
        block_vals = lax.dot_general(coeffs, tile_vals, (((1,), (1,)), ((), ())), precision=highest)
        accumulated = accumulated + lax.dot_general(
            block_data[3:], tile_vals, (((1,), (0,)), ((), ())), precision=highest
        )
        return (accumulated, block_vals)

    accumulated, block_out = lax.scan(
        tile_step, jnp.zeros((3, centres.shape[1]), jnp.float32), blocks
    )
    values = jnp.transpose(block_out, (1, 0, 2)).reshape(3, total_rows)
    back_values = lax.all_to_all(values, "dev", split_axis=1, concat_axis=1, tiled=True)
    own_values = jnp.take(back_values, point_slot, axis=1)
    fluid_disp = jnp.sum((own_values * weight_flat[None, :]).reshape(3, -1, SLOTS), axis=2)
    patch_load = apply_inverse(accumulated, inverse)
    load_term = jnp.zeros((3, node_count * devices), jnp.float32).at[:, node_ids].add(patch_load)
    node_loads = lax.psum_scatter(load_term, "dev", scatter_dimension=1, tiled=True)
    return (fluid_disp, node_loads)


def solution(mesh):
    placed = (
        P(None, "dev"),
        P(None, "dev"),
        P("dev", None),
        P("dev", None, None),
        P(None, "dev"),
        P(None, "dev"),
        P("dev", None),
        P("dev", None),
    )
    return jax.shard_map(
        local,
        mesh=mesh,
        in_specs=placed,
        out_specs=(P(None, "dev"), P(None, "dev")),
        check_vma=False,
    )
```

profile of v0, /device:TPU:0, one launch (start us, length us, event | category | flops | bytes accessed | tf_op | source)
XLA Modules:
  0.0 1353.6 jit_solution(14049836181310177835)
XLA Ops:
  28.0 56.1 %gather_fusion.1 = f32[16384,3]{1,0:T(8,128)} fusion(f32[3,4096]{0,1:T(8,128)} %copy.77, s32[16384]{0:T(1024)S(1)} %broadcast_clamp_fusion.1), kind=kCustom, calls=%fused_computation.1 | custom fusion | bytes 458752 | tf_op jit(solution)/shard_map/gather | solution.py:55
  98.5 56.2 %gather_fusion = f32[16384,3]{1,0:T(8,128)} fusion(f32[3,4096]{0,1:T(8,128)} %copy.75, s32[16384]{0:T(1024)S(1)} %broadcast_clamp_fusion.1), kind=kCustom, calls=%fused_computation | custom fusion | bytes 458752 | tf_op jit(solution)/shard_map/gather | solution.py:55
  196.0 47.4 %scatter_custom_fusion = f32[6,32768]{0,1:T(8,128)} fusion(s32[16384]{0:T(1024)S(1)} %bitcast.99, f32[16384,6]{1,0:T(8,128)} %copy.80, f32[]{:T(128)} %constant.73.clone.1), kind=kCustom, calls=%fused_computation.48 | custom fusion | bytes 786944 | tf_op jit(solution)/shard_map/scatter | solution.py:57
  253.5 11.4 all-to-all-start
  272.3 11.8 all-to-all-done
  286.5 14.5 %gather_fusion.2 = f32[1024,6]{1,0:T(8,128)} fusion(f32[6,65536]{0,1:T(8,128)} %all-gather.2.cloned.1.call-done, s32[1024]{0:T(1024)S(1)} %broadcast_clamp_fusion.2), kind=kCustom, calls=%fused_computation.2 | custom fusion | bytes 53248 | tf_op jit(solution)/shard_map/jit(_take)/gather | solution.py:44
  312.6 298.2 %while.13 = (s32[]{:T(128)}, f32[3,1024]{1,0:T(4,128)S(1)}, f32[16,3,2048]{2,1,0:T(4,128)}, f32[16,6,2048]{2,0,1:T(8,128)S(1)}, f32[3,1024]{1,0:T(4,128)S(1)}, /...) while((s32[]{:T(128)}, f32[3,1024]{1,0:T(4,128)S(1)}, ...), condition=%wide.region_6.7_spmd.clone, body=%wide.region_5.6_spmd.clone.sunk | while | flops 197138432 | bytes 291003 | solution.py:71
  320.4 11.2 fusion.62
  339.0 11.2 fusion.62
  357.6 11.2 fusion.62
  376.2 11.2 fusion.62
  394.8 11.2 fusion.62
  413.4 11.2 fusion.62
  469.2 11.2 fusion.62
  487.8 11.2 fusion.62
  525.1 11.2 fusion.62
  543.7 11.2 fusion.62
  562.3 11.2 fusion.62
  580.9 11.2 fusion.62
  599.5 11.2 fusion.62
  625.7 19.2 %scatter_custom_fusion.1 = f32[3,65536]{0,1:T(8,128)} fusion(s32[1024]{0:T(1024)S(1)} %bitcast.116, f32[1024,3]{1,0:T(8,128)S(1)} %copy.90, f32[]{:T(128)} %constant.73.clone.1), kind=kCustom, calls=%fused_computation.41 | custom fusion | flops 3072 | bytes 786436 | tf_op jit(solution)/shard_map/scatter-add | solution.py:79
  653.3 60.3 %gather_fusion.3 = f32[16384,3]{1,0:T(8,128)} fusion(f32[3,32768]{0,1:T(8,128)} %bitcast.92, s32[16384]{0:T(1024)S(1)} %broadcast_clamp_fusion), kind=kCustom, calls=%fused_computation.3 | custom fusion | bytes 458752 | tf_op jit(solution)/shard_map/jit(_take)/gather | solution.py:76
  713.7 25.6 %multiply_reduce_fusion = f32[3,4096]{0,1:T(8,128)} fusion(f32[3,4096,4]{0,2,1:T(4,128)} %bitcast.93, f32[4096,4]{1,0:T(8,128)S(1)} %copy.76, pred[4096,4]{1,0:T(8,128)(4,1)S(1)} %copy-done.1), kind=kLoop, calls=%fused_computation.47 | loop fusion | flops 135168 | bytes 327680 | tf_op jit(solution)/shard_map/reduce_sum | solution.py:77
  742.1 602.8 %reduce-scatter.2.cloned.1.call-done = f32[3,512]{0,1:T(8,128)} async-done(((f32[3,65536]{0,1:T(8,128)}), f32[3,512]{0,1:T(8,128)}) %reduce-scatter.2.cloned.1.call-update) | async-done | bytes 6160 | tf_op jit(solution)/shard_map/reduce_scatter | solution.py:80
  (141 shorter events, 287.5 us)
Async XLA Ops:
  7.2 16.8 %copy-start.3 = (f32[3,4096]{1,0:T(4,128)S(1)}, f32[3,4096]{1,0:T(4,128)}, u32[]{:S(2)}) copy-start(f32[3,4096]{1,0:T(4,128)} %param.14) | copy-start | bytes 147460
  7.2 279.3 %all-gather.2.cloned.1.call-start = ((), (), s32[]{:S(2)}) async-start(), calls=%async_computation.3 | async-start | bytes 33816576 | tf_op jit(solution)/shard_map/all_gather | solution.py:43
  9.8 16.3 %copy-start.4 = (f32[3,4096]{1,0:T(4,128)S(1)}, f32[3,4096]{1,0:T(4,128)}, u32[]{:S(2)}) copy-start(f32[3,4096]{1,0:T(4,128)} %param.15) | copy-start | bytes 147460
  161.2 3.2 copy-start
  243.4 27.2 %copy-start.5 = (s32[1,1024]{1,0:T(1,128)S(1)}, s32[1,1024]{1,0:T(1,128)}, u32[]{:S(2)}) copy-start(s32[1,1024]{1,0:T(1,128)} %param.12) | copy-start | bytes 12292
  243.4 27.3 %copy-start.2 = (s32[4096,4]{0,1:T(4,128)S(1)}, s32[4096,4]{0,1:T(4,128)}, u32[]{:S(2)}) copy-start(s32[4096,4]{0,1:T(4,128)} %param.16) | copy-start | bytes 196612
  253.5 30.6 %all-to-all-start = ((f32[6,128,256]{2,0,1:T(8,128)}), f32[6,128,256]{2,0,1:T(8,128)S(1)}, u32[]{:S(2)}, u32[]{:S(2)}) async-start(f32[6,128,256]{2,0,1:T(8,128)} %copy.81), calls=%async_computation | async-start | bytes 2097152 | tf_op jit(solution)/shard_map/all_to_all | solution.py:58
  610.8 34.1 %all-to-all-start.1 = ((f32[3,128,256]{2,0,1:T(4,128)}), f32[3,128,256]{2,0,1:T(4,128)S(1)}, u32[]{:S(2)}, u32[]{:S(2)}) async-start(f32[3,128,256]{2,0,1:T(4,128)} %bitcast.98), calls=%async_computation.1 | async-start | bytes 1048576 | tf_op jit(solution)/shard_map/all_to_all | solution.py:75
  615.4 729.5 %reduce-scatter.2.cloned.1.call-start = ((), (), s32[]{:S(2)}) async-start(), calls=%async_computation.4 | async-start | bytes 33816576 | tf_op jit(solution)/shard_map/reduce_scatter | solution.py:80
  644.9 68.8 %copy-start.1 = (pred[4096,4]{1,0:T(8,128)(4,1)S(1)}, pred[4096,4]{1,0:T(8,128)(4,1)}, u32[]{:S(2)}) copy-start(pred[4096,4]{1,0:T(8,128)(4,1)} %copy.73) | copy-start | bytes 49156
Sparse Core Ops, SparseCore 0:
  11.0 108.8 all-gather.1
  645.0 699.8 reduce-scatter.1
where the time goes:
time: 1360 us; the launch traced here: 1350 us
  waiting for transfers between devices  615 us (45%)
  matrix products  316 us (23%)
  local copies, waits for them, and re-layouts  315 us (23%)
  other arithmetic  75.7 us (6%)
  starting transfers between devices  16.2 us (1%)
  between operations  14.5 us (1%)
    reduce_scatter x1, waiting for transfers between devices, local(): lax.psum_scatter(load_term, 'dev', scatter_dimension=1, tiled=True)  603 us
    dot_general x16, matrix products, tile_step(): lax.dot_general(coeffs, tile_vals, (((1,), (1,)), ((), ())), precision=hi...  179 us
    dot_general x16, matrix products, tile_step(): lax.dot_general(block_data[3:], tile_vals, (((1,), (0,)), ((), ())), prec...  117 us
    gather x2, local copies, waits for them, and re-layouts, local(): fluid_coords[:, point_row]  61.7 us
    gather x1, local copies, waits for them, and re-layouts, local(): own_values = jnp.take(back_values, point_slot, axis=1)  60.3 us
    gather x1, local copies, waits for them, and re-layouts, local(): fluid_loads[:, point_row]  56.1 us
    scatter x1, local copies, waits for them, and re-layouts, local(): jnp.zeros((6, devices * bucket), jnp.float32).at[:, point_slot].set(payload)  47.4 us
  transfers between devices with their start and end apart: 4, of which 2 were waited for; matrix products, arithmetic and copies ran while one was open for 28% of the time, Pallas kernels for 0%

commit v1 on v0

v1 whole, which is shorter than its diff:
```python
import jax
import jax.numpy as jnp
from jax import lax
from jax.experimental import pallas as pl
from jax.experimental.pallas import tpu as pltpu
from jax.sharding import PartitionSpec as P

PN = 1024
SLOTS = 4
PATCHES = 128
NODE_DEV = 512
LANES = 128
SIDE = 4
STRIDE = (32, 8, 2)
GAIN = 8.0

f32 = jnp.float32
bf16 = jnp.bfloat16
VMEM = pltpu.VMEM
MESH = pl.DeviceIdType.MESH


def place():
    me = lax.axis_index("dev")
    return me, lax.rem(me, 2), tuple(lax.rem(me // s, SIDE) for s in STRIDE)


def peer_of(me, spot, axis, step):
    return me + (lax.rem(spot[axis] + step, SIDE) - spot[axis]) * STRIDE[axis]


def meet(me, core, spot):
    barrier = pltpu.get_barrier_semaphore()
    for axis in range(3):
        for step in (1, 2, 3):
            peer = peer_of(me, spot, axis, step)
            pl.semaphore_signal(barrier, inc=1, device_id=(peer,), device_id_type=MESH)
    pl.semaphore_signal(barrier, inc=1, device_id=(me + 1 - 2 * core,), device_id_type=MESH)
    pl.semaphore_wait(barrier, 10)


def send(src, dst, send_sem, recv_sem, device):
    copy = pltpu.make_async_remote_copy(
        src_ref=src,
        dst_ref=dst,
        send_sem=send_sem,
        recv_sem=recv_sem,
        device_id=(device,),
        device_id_type=MESH,
    )
    copy.start()
    return copy


def gather_stages(out, place_now, sems):
    me, core, spot = place_now
    send_sem, recv_sem, core_send, core_recv = sems
    for stage in range(3):
        copies = []
        for g in range(3):
            axis = (g + stage) % 3
            done = [(g + t) % 3 for t in range(stage)]
            where = tuple(slice(None) if a in done else spot[a] for a in range(3)) + (core, g)
            for step in (1, 2, 3):
                part = out.at[where]
                copies.append(
                    send(
                        part,
                        part,
                        send_sem.at[stage, g, step - 1],
                        recv_sem.at[stage, g, 3 - step],
                        peer_of(me, spot, axis, step),
                    )
                )
        for copy in copies:
            copy.wait()
    part = out.at[:, :, :, core]
    send(part, part, core_send, core_recv, me + 1 - 2 * core).wait()


def sum_kernel(terms, out, core_in, s1, r2, s2, r3, s3, r4, send_sem, recv_sem, core_send, core_recv):
    me, core, spot = place()
    meet(me, core, spot)
    part = terms.at[:, :, :, 1 - core]
    send(part, core_in, core_send, core_recv, me + 1 - 2 * core).wait()
    for a in range(SIDE):
        for g in range(3):
            s1[g, a] = terms[a, :, :, core, g] + core_in[a, :, :, g]
    sums, landed = (s1, s2, s3), (r2, r3, r4)
    for stage in range(3):
        src, dst = sums[stage], landed[stage]
        ahead = []
        for g in range(3):
            gone = [(g + t) % 3 for t in range(stage)]
            ahead.append([a for a in range(3) if a not in gone].index((g + stage) % 3))
        copies = []
        for g in range(3):
            axis = (g + stage) % 3
            for step in (1, 2, 3):
                to = lax.rem(spot[axis] + step, SIDE)
                copies.append(
                    send(
                        src.at[(g,) + (slice(None),) * ahead[g] + (to,)],
                        dst.at[g, 3 - step],
                        send_sem.at[stage, g, step - 1],
                        recv_sem.at[stage, g, 3 - step],
                        peer_of(me, spot, axis, step),
                    )
                )
        for g in range(3):
            axis = (g + stage) % 3
            for k in range(3):
                copies[3 * g + k].wait_recv()
            mine = (g,) + (slice(None),) * ahead[g] + (spot[axis],)
            total = (src[mine] + dst[g, 0]) + (dst[g, 1] + dst[g, 2])
            if stage < 2:
                sums[stage + 1][g] = total
            else:
                out[g] = total
        for copy in copies:
            copy.wait_send()


def sum_scatter(terms, collective_id):
    tail = terms.shape[5:]
    dma = pltpu.SemaphoreType.DMA
    return pl.pallas_call(
        sum_kernel,
        out_shape=jax.ShapeDtypeStruct((3,) + tail, f32),
        in_specs=[pl.BlockSpec(memory_space=VMEM)],
        out_specs=pl.BlockSpec(memory_space=VMEM),
        scratch_shapes=[
            VMEM((4, 4, 4, 3) + tail, f32),
            VMEM((3, 4, 4, 4) + tail, f32),
            VMEM((3, 3, 4, 4) + tail, f32),
            VMEM((3, 4, 4) + tail, f32),
            VMEM((3, 3, 4) + tail, f32),
            VMEM((3, 4) + tail, f32),
            VMEM((3, 3) + tail, f32),
            dma((3, 3, 3)),
            dma((3, 3, 3)),
            dma,
            dma,
        ],
        compiler_params=pltpu.CompilerParams(collective_id=collective_id, has_side_effects=True),
    )(terms)


def node_kernel(coords, disp, out, *sems):
    me, core, spot = place()
    for g in range(3):
        for r in range(4):
            lanes = pl.ds(r * LANES, LANES)
            out[spot[0], spot[1], spot[2], core, g, pl.ds(r, 1), :] = coords[pl.ds(g, 1), lanes]
            out[spot[0], spot[1], spot[2], core, g, pl.ds(4 + r, 1), :] = disp[pl.ds(g, 1), lanes]
    meet(me, core, spot)
    gather_stages(out, (me, core, spot), sems)


def patch_kernel(rows, out, own_sem, *sems):
    me, core, spot = place()
    own = pltpu.make_async_copy(rows, out.at[spot[0], spot[1], spot[2], core], own_sem)
    own.start()
    meet(me, core, spot)
    own.wait()
    gather_stages(out, (me, core, spot), sems)


def gather_call(kernel, args, rows, own, collective_id):
    dma = pltpu.SemaphoreType.DMA
    return pl.pallas_call(
        kernel,
        out_shape=jax.ShapeDtypeStruct((4, 4, 4, 2, 3, rows, LANES), f32),
        in_specs=[pl.BlockSpec(memory_space=VMEM)] * len(args),
        out_specs=pl.BlockSpec(memory_space=VMEM),
        scratch_shapes=[dma] * own + [dma((3, 3, 3)), dma((3, 3, 3)), dma, dma],
        compiler_params=pltpu.CompilerParams(collective_id=collective_id, has_side_effects=True),
    )(*args)


def halves(x):
    high = x.astype(bf16)
    return high, (x - high.astype(f32)).astype(bf16)


def times_factor(values, high, low, contract):
    top, bottom = halves(values)
    both = jnp.concatenate([top, bottom], axis=0)
    dims = (((1,), (contract,)), ((), ()))
    first = lax.dot_general(both, high, dims, preferred_element_type=f32)
    second = lax.dot_general(both, low, dims, preferred_element_type=f32)
    return (first[:8] + first[8:]) + (second[:8] + second[8:])


def apply_inverse(values, high, low):
    return times_factor(times_factor(values, high, low, 1), high, low, 0)


def owners(ids):
    device = lax.shift_right_logical(ids, 9)
    local = lax.bitwise_and(ids, NODE_DEV - 1)
    at_device = lax.broadcasted_iota(jnp.int32, (PATCHES, PN), 0) == device
    at_local = lax.broadcasted_iota(jnp.int32, (NODE_DEV, PN), 0) == local
    return at_device, jnp.where(at_local, 1.0, 0.0).astype(bf16)


def coeff_kernel(table, ids, factor, out):
    at_device, at_local = owners(ids[...])
    pieces = []
    for g in range(3):
        for h in range(2):
            row = [table[pl.ds(8 * g + 4 * h + r, PATCHES, stride=24), :] for r in range(4)]
            pieces.append(jnp.concatenate(row, axis=1))
    stacked = jnp.concatenate(pieces, axis=0)
    high, low = halves(stacked)
    found = jnp.dot(high, at_local, preferred_element_type=f32)
    found = found + jnp.dot(low, at_local, preferred_element_type=f32)
    picked = []
    for c in range(6):
        mine = found[c * PATCHES : (c + 1) * PATCHES]
        picked.append(jnp.sum(jnp.where(at_device, mine, 0.0), axis=0, keepdims=True))
    moved = jnp.concatenate([picked[1], picked[3], picked[5]] + [jnp.zeros((5, PN), f32)], axis=0)
    coeffs = apply_inverse(moved, *halves(factor[...]))
    for g in range(3):
        scaled = picked[2 * g] * (-2.0 * GAIN)
        for s in range(8):
            lanes = slice(s * LANES, (s + 1) * LANES)
            out[g, pl.ds(s, 1), :] = scaled[:, lanes]
            out[g, pl.ds(8 + s, 1), :] = coeffs[g : g + 1, lanes]


def load_kernel(summed, ids, factor, out):
    rows = jnp.concatenate([summed[:, s, :] for s in range(8)], axis=1)
    rows = jnp.concatenate([rows, jnp.zeros((5, PN), f32)], axis=0)
    loads = apply_inverse(rows * (1.0 / 32.0), *halves(factor[...]))
    at_device, at_local = owners(ids[...])
    parts = []
    for g in range(3):
        parts.extend(halves(jnp.where(at_device, loads[g : g + 1], 0.0)))
    terms = lax.dot_general(
        jnp.concatenate(parts, axis=0),
        at_local,
        (((1,), (1,)), ((), ())),
        preferred_element_type=f32,
    )
    for g in range(3):
        base = 2 * g * PATCHES
        term = terms[base : base + PATCHES] + terms[base + PATCHES : base + 2 * PATCHES]
        for r in range(4):
            lanes = slice(r * LANES, (r + 1) * LANES)
            out[pl.ds(4 * g + r, PATCHES, stride=12), :] = term[:, lanes]


def in_vmem(kernel, args, shape):
    return pl.pallas_call(
        kernel,
        out_shape=jax.ShapeDtypeStruct(shape, f32),
        in_specs=[pl.BlockSpec(memory_space=VMEM)] * len(args),
        out_specs=pl.BlockSpec(memory_space=VMEM),
        compiler_params=pltpu.CompilerParams(vmem_limit_bytes=56 * 2**20),
    )(*args)


def fold_rows(regs, masks):
    for shift, mask in zip((4, 2, 1), masks):
        n = len(regs) // 2
        out = []
        for a, b in zip(regs[:n], regs[n:]):
            if shift == 4:
                out.append(jnp.where(mask, a, b) + pltpu.roll(jnp.where(mask, b, a), 4, 0))
            else:
                left, right = pltpu.roll(a, 8 - shift, 0), pltpu.roll(b, shift, 0)
                out.append(jnp.where(mask, a, b) + jnp.where(mask, left, right))
        regs = out
    return regs[0]


FIELDS = 11


def fluid_kernel(patch, coords, loads, blend, table, disp, acc, norm, record, wide, sums):
    points = coords.shape[1]
    acc[...] = jnp.zeros_like(acc)
    row = lax.broadcasted_iota(jnp.int32, (8, LANES), 0)
    masks = [(row & bit) == 0 for bit in (4, 2, 1)]

    def patch_step(p, _):
        y = [table[6 * p + 2 * c] for c in range(3)]
        total = (y[0] * y[0] + y[1] * y[1]) + y[2] * y[2]
        norm[p] = 1.0 + total * (1.0 / (4.0 * GAIN))
        return 0

    lax.fori_loop(0, PATCHES, patch_step, 0)

    def record_step(j, _):
        lanes = pl.ds(pl.multiple_of(j * LANES, LANES), LANES)
        x, b = coords[:, lanes], blend[:, lanes]
        square = GAIN * jnp.sum(x * x, axis=0, keepdims=True)
        share = b / jnp.sum(b, axis=0, keepdims=True)
        field = jnp.concatenate([x, loads[:, lanes], square, share, jnp.zeros((5, LANES), f32)], axis=0)
        record[lanes, pl.ds(0, 16)] = field.T
        return 0

    lax.fori_loop(0, points // LANES, record_step, 0)

    def spread(group, slot):
        block = record[pl.ds(pl.multiple_of(group * 8, 8), 8), :]
        for j in range(FIELDS):
            wide[slot * FIELDS + j] = jnp.broadcast_to(block[:, j : j + 1], (8, LANES))

    groups = points // 8
    spread(0, 0)

    def point_step(group, _):
        first = pl.multiple_of(group * 8, 8)
        slot = lax.rem(group, 2)
        spread(jnp.minimum(group + 1, groups - 1), 1 - slot)
        names = [patch.at[s, pl.ds(first, 8)] for s in range(SLOTS)]
        value = [[], [], []]
        for q in range(8):

            def field(j):
                return wide[slot * FIELDS + j, pl.ds(q, 8, stride=0), :]

            x, y, z, square = field(0), field(1), field(2), field(6)
            force = [field(3 + c) for c in range(3)]
            ps = [names[s][q] for s in range(SLOTS)]
            term = []
            for s in range(SLOTS):
                p = ps[s]
                near = (table[6 * p] * x + table[6 * p + 2] * y) + (
                    table[6 * p + 4] * z + (norm[p] + square)
                )
                term.append(lax.rsqrt(near) * field(7 + s))
            old = [[acc[3 * p + c] for c in range(3)] for p in ps]
            for c in range(3):
                dots = [table[6 * ps[s] + 2 * c + 1] * term[s] for s in range(SLOTS)]
                value[c].append((dots[0] + dots[1]) + (dots[2] + dots[3]))
            for s in range(SLOTS):
                for c in range(3):
                    acc[3 * ps[s] + c] = old[s][c] + term[s] * force[c]
        for c in range(3):
            sums[c, pl.ds(first, 8), :] = fold_rows(value[c], masks)
        return 0

    lax.fori_loop(0, groups, point_step, 0)

    def out_step(j, _):
        lanes = pl.ds(pl.multiple_of(j * LANES, LANES), LANES)
        for c in range(3):
            disp[pl.ds(c, 1), lanes] = jnp.sum(sums[c, lanes, :].T, axis=0, keepdims=True) * (1.0 / 32.0)
        return 0

    lax.fori_loop(0, points // LANES, out_step, 0)


def fluid(patch, coords, loads, blend, table):
    points = coords.shape[1]
    return pl.pallas_call(
        fluid_kernel,
        out_shape=(
            jax.ShapeDtypeStruct((3, points), f32),
            jax.ShapeDtypeStruct((PATCHES * 3, 8, LANES), f32),
        ),
        in_specs=[pl.BlockSpec(memory_space=pltpu.SMEM)] + [pl.BlockSpec(memory_space=VMEM)] * 4,
        out_specs=[pl.BlockSpec(memory_space=VMEM)] * 2,
        scratch_shapes=[
            VMEM((PATCHES, 8, LANES), f32),
            VMEM((points, LANES), f32),
            VMEM((2 * FIELDS, 8, LANES), f32),
            VMEM((3, points, LANES), f32),
        ],
    )(patch, coords, loads, blend, table)


def local(node_coords, node_disp, node_list, factor, fluid_coords, fluid_loads, fluid_patch, blend_raw):
    inverse = factor[0]
    nodes = gather_call(node_kernel, (node_coords, node_disp), 8, 0, 0)
    nodes = nodes.reshape(PATCHES * 24, LANES)
    rows = in_vmem(coeff_kernel, (nodes, node_list, inverse), (3, 16, LANES))
    table = gather_call(patch_kernel, (rows,), 16, 1, 1)
    table = table.reshape(PATCHES * 6, 8, LANES)
    fluid_disp, terms = fluid(fluid_patch.T, fluid_coords, fluid_loads, blend_raw.T, table)
    summed = sum_scatter(terms.reshape(4, 4, 4, 2, 3, 8, LANES), 2)
    spread = in_vmem(load_kernel, (summed, node_list, inverse), (PATCHES * 12, LANES))
    owned = sum_scatter(spread.reshape(4, 4, 4, 2, 3, 4, LANES), 3)
    return fluid_disp, owned.reshape(3, NODE_DEV)


def solution(mesh):
    placed = (
        P(None, "dev"),
        P(None, "dev"),
        P("dev", None),
        P("dev", None, None),
        P(None, "dev"),
        P(None, "dev"),
        P("dev", None),
        P("dev", None),
    )
    return jax.shard_map(
        local,
        mesh=mesh,
        in_specs=placed,
        out_specs=(P(None, "dev"), P(None, "dev")),
        check_vma=False,
    )
```

time: 1360 us -> 236 us (0.17)
  waiting for transfers between devices: 615 us -> 0 us
  matrix products: 316 us -> 0 us
  local copies, waits for them, and re-layouts: 315 us -> 1.29 us
  Pallas kernels: 0 us -> 234 us
  other arithmetic: 75.7 us -> 0 us
  starting transfers between devices: 16.2 us -> 0 us
  between operations: 14.5 us -> 0.66 us
    reduce_scatter x1 -> x0, waiting for transfers between devices: 603 us -> none  [local(): lax.psum_scatter(load_term, 'dev', scatter_dimension=1, tiled=True)]
    dot_general x36 -> x0, matrix products: 316 us -> none  [the longest x16 179 us: tile_step(): lax.dot_general(coeffs, tile_vals, (((1,), (1,)), ((), ())), precision=hi...]
    pallas_call x0 -> x7, Pallas kernels: none -> 234 us  [the longest x1 140 us: fluid(): pl.pallas_call(fluid_kernel, out_shape=(jax.ShapeDtypeStruct((3, points),...]
    gather x5 -> x0, local copies, waits for them, and re-layouts: 193 us -> none  [the longest x2 61.7 us: local(): fluid_coords[:, point_row]]
    scatter x1 -> x0, local copies, waits for them, and re-layouts: 47.4 us -> none  [local(): jnp.zeros((6, devices * bucket), jnp.float32).at[:, point_slot].set(payload)]
    reduce_sum x3 -> x0, other arithmetic: 34.7 us -> none  [the longest x1 25.6 us: local(): jnp.sum((own_values * weight_flat[None, :]).reshape(3, -1, SLOTS), axis=2)]
    all_to_all x3 -> x0, local copies, waits for them, and re-layouts: 19.7 us -> none  [the longest x2 11.2 us: local(): lax.all_to_all(send_points, 'dev', split_axis=1, concat_axis=1, tiled=True)]
    scatter-add x1 -> x0, other arithmetic: 19.2 us -> none  [local(): jnp.zeros((3, node_count * devices), jnp.float32).at[:, node_ids]]
  transfers between devices with their start and end apart: 4 -> 0, of which waited for: 2 -> 0; matrix products, arithmetic and copies ran while one was open for 28% -> 0% of each run, Pallas kernels for 0% -> 0%
where the time goes in v1:
time: 236 us
  Pallas kernels  234 us (99%)
    pallas_call x1, Pallas kernels, fluid(): pl.pallas_call(fluid_kernel, out_shape=(jax.ShapeDtypeStruct((3, points),...  140 us
    pallas_call x2, Pallas kernels, gather_call(): pl.pallas_call(kernel, out_shape=jax.ShapeDtypeStruct((4, 4, 4, 2, 3, row...  45.1 us
    pallas_call x2, Pallas kernels, sum_scatter(): pl.pallas_call(sum_kernel, out_shape=jax.ShapeDtypeStruct((3,) + tail, f3...  36.5 us
    pallas_call x2, Pallas kernels, in_vmem(): pl.pallas_call(kernel, out_shape=jax.ShapeDtypeStruct(shape, f32), in_spe...  12.6 us

profile of v1, /device:TPU:0, one launch (start us, length us, event | category | flops | bytes accessed | tf_op | source)
XLA Modules:
  0.0 236.1 jit_solution(2864839296273885385)
XLA Ops:
  0.6 22.8 %shard_map.95 = f32[4,4,4,2,3,8,128]{6,5,4,3,2,1,0:T(8,128)} custom-call(f32[3,512]{1,0:T(4,128)} %coords.2, f32[3,512]{1,0:T(4,128)} %disp.1), custom_call_target="tpu_custom_call" | custom-call | tf_op jit(solution)/shard_map/pallas_call | solution.py:171
  23.4 6.8 %shard_map.96.rows = f32[3,16,128]{2,1,0:T(8,128)} custom-call(f32[3072,128]{1,0:T(8,128)} %bitcast.14, s32[1,1024]{1,0:T(1,128)} %ids.3, f32[1024,1024]{1,0:T(8,128)} %bitcast.11), custom_call_target="tpu_custom_call" | custom-call | tf_op jit(solution)/shard_map/pallas_call | solution.py:255
  30.3 22.3 %shard_map.97 = f32[4,4,4,2,3,16,128]{6,5,4,3,2,1,0:T(8,128)} custom-call(f32[3,16,128]{2,1,0:T(8,128)} %shard_map.96.rows), custom_call_target="tpu_custom_call" | custom-call | tf_op jit(solution)/shard_map/pallas_call | solution.py:171
  52.6 139.9 %shard_map.98 = (f32[3,4096]{1,0:T(4,128)}, f32[384,8,128]{2,1,0:T(8,128)}) custom-call(s32[4,4096]{1,0:T(4,128)} %bitcast.17, f32[3,4096]{1,0:T(4,128)} %coords.3, f32[3,4096]{1,0:T(4,128)} %loads.1, f32[4,4096]{1,0:T(4,128)} %bitcast.18, f32[768,8,128]{2,1,0:T(8,128)} %bitcast.13), custom_call_target="tpu_custom_call" | custom-call | tf_op jit(solution)/shard_map/pallas_call | solution.py:359
  192.5 19.6 %shard_map.99.summed = f32[3,8,128]{2,1,0:T(8,128)} custom-call(f32[4,4,4,2,3,8,128]{6,5,4,3,2,1,0:T(8,128)} %bitcast.16), custom_call_target="tpu_custom_call" | custom-call | tf_op jit(solution)/shard_map/pallas_call | solution.py:127
  212.1 5.8 %shard_map.100 = f32[1536,128]{1,0:T(8,128)} custom-call(f32[3,8,128]{2,1,0:T(8,128)} %shard_map.99.summed, s32[1,1024]{1,0:T(1,128)} %ids.3, f32[1024,1024]{1,0:T(8,128)} %bitcast.12), custom_call_target="tpu_custom_call" | custom-call | tf_op jit(solution)/shard_map/pallas_call | solution.py:255
  217.9 16.9 %shard_map.101 = f32[3,4,128]{2,1,0:T(4,128)} custom-call(f32[4,4,4,2,3,4,128]{6,5,4,3,2,1,0:T(4,128)} %bitcast.15), custom_call_target="tpu_custom_call" | custom-call | tf_op jit(solution)/shard_map/pallas_call | solution.py:127
  234.8 1.3 copy.12

commit v2 on v1

v2 whole, which is shorter than its diff:
```python
import jax
import jax.numpy as jnp
from jax import lax
from jax.experimental import pallas as pl
from jax.experimental.pallas import tpu as pltpu
from jax.sharding import PartitionSpec as P

PN = 1024
SLOTS = 4
PATCHES = 128
NODE_DEV = 512
LANES = 128
SIDE = 4
STRIDE = (32, 8, 2)
GAIN = 8.0

f32 = jnp.float32
bf16 = jnp.bfloat16
VMEM = pltpu.VMEM
MESH = pl.DeviceIdType.MESH


def place():
    me = lax.axis_index("dev")
    return me, lax.rem(me, 2), tuple(lax.rem(me // s, SIDE) for s in STRIDE)


def peer_of(me, spot, axis, step):
    return me + (lax.rem(spot[axis] + step, SIDE) - spot[axis]) * STRIDE[axis]


def greet(me, core, spot):
    barrier = pltpu.get_barrier_semaphore()
    for axis in range(3):
        for step in (1, 2, 3):
            peer = peer_of(me, spot, axis, step)
            pl.semaphore_signal(barrier, inc=1, device_id=(peer,), device_id_type=MESH)
    pl.semaphore_signal(barrier, inc=1, device_id=(me + 1 - 2 * core,), device_id_type=MESH)
    return barrier


def send(src, dst, send_sem, recv_sem, device):
    copy = pltpu.make_async_remote_copy(
        src_ref=src,
        dst_ref=dst,
        send_sem=send_sem,
        recv_sem=recv_sem,
        device_id=(device,),
        device_id_type=MESH,
    )
    copy.start()
    return copy


def nothing():
    pass


def gather_stages(out, place_now, sems, beside):
    me, core, spot = place_now
    send_sem, recv_sem, core_send, core_recv = sems
    for stage in range(3):
        copies = []
        for g in range(3):
            axis = (g + stage) % 3
            done = [(g + t) % 3 for t in range(stage)]
            where = tuple(slice(None) if a in done else spot[a] for a in range(3)) + (core, g)
            for step in (1, 2, 3):
                part = out.at[where]
                copies.append(
                    send(
                        part,
                        part,
                        send_sem.at[stage, g, step - 1],
                        recv_sem.at[stage, g, 3 - step],
                        peer_of(me, spot, axis, step),
                    )
                )
        beside[stage]()
        for copy in copies:
            copy.wait()
    part = out.at[:, :, :, core]
    send(part, part, core_send, core_recv, me + 1 - 2 * core).wait()


def sum_stages(terms, place_now, buffers, sems):
    me, core, spot = place_now
    core_in, s1, r2, s2, r3, s3, r4 = buffers
    send_sem, recv_sem, core_send, core_recv = sems
    part = terms.at[:, :, :, 1 - core]
    send(part, core_in, core_send, core_recv, me + 1 - 2 * core).wait()
    for a in range(SIDE):
        for g in range(3):
            s1[g, a] = terms[a, :, :, core, g] + core_in[a, :, :, g]
    sums, landed = (s1, s2, s3), (r2, r3, r4)
    totals = []
    for stage in range(3):
        src, dst = sums[stage], landed[stage]
        ahead = []
        for g in range(3):
            gone = [(g + t) % 3 for t in range(stage)]
            ahead.append([a for a in range(3) if a not in gone].index((g + stage) % 3))
        copies = []
        for g in range(3):
            axis = (g + stage) % 3
            for step in (1, 2, 3):
                to = lax.rem(spot[axis] + step, SIDE)
                copies.append(
                    send(
                        src.at[(g,) + (slice(None),) * ahead[g] + (to,)],
                        dst.at[g, 3 - step],
                        send_sem.at[stage, g, step - 1],
                        recv_sem.at[stage, g, 3 - step],
                        peer_of(me, spot, axis, step),
                    )
                )
        for g in range(3):
            axis = (g + stage) % 3
            for k in range(3):
                copies[3 * g + k].wait_recv()
            mine = (g,) + (slice(None),) * ahead[g] + (spot[axis],)
            total = (src[mine] + dst[g, 0]) + (dst[g, 1] + dst[g, 2])
            if stage < 2:
                sums[stage + 1][g] = total
            else:
                totals.append(total)
        for copy in copies:
            copy.wait_send()
    return totals


def sum_buffers(rows):
    tail = (rows, LANES)
    return [
        VMEM((4, 4, 4, 3) + tail, f32),
        VMEM((3, 4, 4, 4) + tail, f32),
        VMEM((3, 3, 4, 4) + tail, f32),
        VMEM((3, 4, 4) + tail, f32),
        VMEM((3, 3, 4) + tail, f32),
        VMEM((3, 4) + tail, f32),
        VMEM((3, 3) + tail, f32),
    ]


def stage_sems():
    dma = pltpu.SemaphoreType.DMA
    return [dma((3, 3, 3)), dma((3, 3, 3)), dma, dma]


def halves(x):
    high = x.astype(bf16)
    return high, (x - high.astype(f32)).astype(bf16)


def times_factor(values, high, low, contract):
    top, bottom = halves(values)
    both = jnp.concatenate([top, bottom], axis=0)
    dims = (((1,), (contract,)), ((), ()))
    first = lax.dot_general(both, high[...], dims, preferred_element_type=f32)
    second = lax.dot_general(both, low[...], dims, preferred_element_type=f32)
    return (first[:8] + first[8:]) + (second[:8] + second[8:])


def apply_inverse(values, high, low):
    return times_factor(times_factor(values, high, low, 1), high, low, 0)


def at_owner(ids):
    device = lax.shift_right_logical(ids[...], 9)
    return lax.broadcasted_iota(jnp.int32, (PATCHES, PN), 0) == device


def mark_local(ids, marks):
    local = lax.bitwise_and(ids[...], NODE_DEV - 1)
    found = lax.broadcasted_iota(jnp.int32, (NODE_DEV, PN), 0) == local
    marks[...] = jnp.where(found, 1.0, 0.0).astype(bf16)


def split_factor(factor, high, low):
    def step(t, _):
        part = pl.ds(pl.multiple_of(t * LANES, LANES), LANES)
        high[part, :], low[part, :] = halves(factor[part, :])
        return 0

    lax.fori_loop(0, PN // LANES, step, 0)


def factor_scratch():
    return [
        VMEM((PN, PN), f32),
        VMEM((PN, PN), bf16),
        VMEM((PN, PN), bf16),
        VMEM((NODE_DEV, PN), bf16),
        pltpu.SemaphoreType.DMA,
    ]


def patch_kernel(coords, disp, ids, factor_hbm, fluid_x, fluid_f, blend, names, *rest):
    table, fields, targets, nodes, factor, high, low, marks, factor_sem = rest[:9]
    node_sems, table_sems = rest[9:13], rest[13:17]
    me, core, spot = place()
    load = pltpu.make_async_copy(factor_hbm, factor, factor_sem)
    load.start()
    barrier = greet(me, core, spot)
    for g in range(3):
        for r in range(4):
            lanes = pl.ds(r * LANES, LANES)
            nodes[spot[0], spot[1], spot[2], core, g, pl.ds(r, 1), :] = coords[pl.ds(g, 1), lanes]
            nodes[spot[0], spot[1], spot[2], core, g, pl.ds(4 + r, 1), :] = disp[pl.ds(g, 1), lanes]
    mark_local(ids, marks)
    pl.semaphore_wait(barrier, 10)

    def fill_fields():
        x, f, b = fluid_x[...], fluid_f[...], blend[...]
        square = GAIN * jnp.sum(x * x, axis=0, keepdims=True)
        share = b / jnp.sum(b, axis=0, keepdims=True)
        for c in range(3):
            fields[c] = x[c : c + 1]
            fields[3 + c] = f[c : c + 1]
        fields[6] = square
        for s in range(SLOTS):
            fields[7 + s] = share[s : s + 1]
            targets[s] = names[pl.ds(s, 1), :]

    def ready_factor():
        load.wait()
        split_factor(factor, high, low)

    gather_stages(nodes, (me, core, spot), node_sems, (fill_fields, ready_factor, nothing))

    rows = nodes.reshape(PATCHES * 24, LANES)

    def pick(h):
        pieces = []
        for g in range(3):
            first = 8 * g + 4 * h
            row = [rows[pl.ds(first + r, PATCHES, stride=24), :] for r in range(4)]
            pieces.append(jnp.concatenate(row, axis=1))
        top, bottom = halves(jnp.concatenate(pieces, axis=0))
        found = jnp.dot(top, marks[...], preferred_element_type=f32)
        found = found + jnp.dot(bottom, marks[...], preferred_element_type=f32)
        where = at_owner(ids)
        out = []
        for g in range(3):
            mine = jnp.where(where, found[g * PATCHES : (g + 1) * PATCHES], 0.0)
            out.append(jnp.sum(mine, axis=0, keepdims=True))
        return out

    moved = jnp.concatenate(pick(1) + [jnp.zeros((5, PN), f32)], axis=0)
    coeffs = apply_inverse(moved, high, low)
    centres = pick(0)
    for g in range(3):
        scaled = centres[g] * (-2.0 * GAIN)
        for s in range(8):
            lanes = slice(s * LANES, (s + 1) * LANES)
            table[spot[0], spot[1], spot[2], core, g, pl.ds(s, 1), :] = scaled[:, lanes]
            table[spot[0], spot[1], spot[2], core, g, pl.ds(8 + s, 1), :] = coeffs[g : g + 1, lanes]
    gather_stages(table, (me, core, spot), table_sems, (nothing,) * 3)


def patch_tables(node_coords, node_disp, node_list, factor, coords, loads, blend, names):
    points = coords.shape[1]
    vmem = pl.BlockSpec(memory_space=VMEM)
    return pl.pallas_call(
        patch_kernel,
        out_shape=(
            jax.ShapeDtypeStruct((4, 4, 4, 2, 3, 16, LANES), f32),
            jax.ShapeDtypeStruct((FIELDS, 1, points), f32),
            jax.ShapeDtypeStruct((SLOTS, 1, points), jnp.int32),
        ),
        in_specs=[vmem] * 3 + [pl.BlockSpec(memory_space=pl.ANY)] + [vmem] * 4,
        out_specs=[vmem] * 3,
        scratch_shapes=[VMEM((4, 4, 4, 2, 3, 8, LANES), f32)]
        + factor_scratch()
        + stage_sems()
        + stage_sems(),
        compiler_params=pltpu.CompilerParams(
            collective_id=0, has_side_effects=True, vmem_limit_bytes=60 * 2**20
        ),
    )(node_coords, node_disp, node_list, factor, coords, loads, blend, names)


def load_kernel(terms, ids, factor_hbm, out, spread, factor, high, low, marks, factor_sem, *rest):
    patch_buffers, node_buffers = rest[:7], rest[7:14]
    patch_sems, node_sems = rest[14:18], rest[18:22]
    me, core, spot = place()
    load = pltpu.make_async_copy(factor_hbm, factor, factor_sem)
    load.start()
    barrier = greet(me, core, spot)
    mark_local(ids, marks)
    load.wait()
    split_factor(factor, high, low)
    pl.semaphore_wait(barrier, 10)
    summed = sum_stages(terms, (me, core, spot), patch_buffers, patch_sems)
    rows = [jnp.concatenate([part[s : s + 1] for s in range(8)], axis=1) for part in summed]
    rows = jnp.concatenate(rows + [jnp.zeros((5, PN), f32)], axis=0)
    loads = apply_inverse(rows * (1.0 / 32.0), high, low)
    where = at_owner(ids)
    parts = []
    for g in range(3):
        parts.extend(halves(jnp.where(where, loads[g : g + 1], 0.0)))
    found = lax.dot_general(
        jnp.concatenate(parts, axis=0),
        marks[...],
        (((1,), (1,)), ((), ())),
        preferred_element_type=f32,
    )
    flat = spread.reshape(PATCHES * 12, LANES)
    for g in range(3):
        base = 2 * g * PATCHES
        term = found[base : base + PATCHES] + found[base + PATCHES : base + 2 * PATCHES]
        for r in range(4):
            lanes = slice(r * LANES, (r + 1) * LANES)
            flat[pl.ds(4 * g + r, PATCHES, stride=12), :] = term[:, lanes]
    owned = sum_stages(spread, (me, core, spot), node_buffers, node_sems)
    for g in range(3):
        for r in range(4):
            out[pl.ds(g, 1), pl.ds(r * LANES, LANES)] = owned[g][r : r + 1]


def node_sums(terms, node_list, factor):
    vmem = pl.BlockSpec(memory_space=VMEM)
    return pl.pallas_call(
        load_kernel,
        out_shape=jax.ShapeDtypeStruct((3, NODE_DEV), f32),
        in_specs=[vmem] * 2 + [pl.BlockSpec(memory_space=pl.ANY)],
        out_specs=vmem,
        scratch_shapes=[VMEM((4, 4, 4, 2, 3, 4, LANES), f32)]
        + factor_scratch()
        + sum_buffers(8)
        + sum_buffers(4)
        + stage_sems()
        + stage_sems(),
        compiler_params=pltpu.CompilerParams(
            collective_id=1, has_side_effects=True, vmem_limit_bytes=60 * 2**20
        ),
    )(terms, node_list, factor)


FIELDS = 11


def fluid_kernel(*refs):
    patch, fields, table, disp, acc, work, sumacc, got = refs[:8]
    names, data = refs[8 : 8 + SLOTS], refs[8 + SLOTS :]
    copies = [pltpu.make_async_copy(patch.at[s], names[s], got.at[s]) for s in range(SLOTS)]
    copies += [pltpu.make_async_copy(fields.at[j], data[j], got.at[SLOTS + j]) for j in range(FIELDS)]
    for copy in copies:
        copy.start()
    points = disp.shape[1]
    lane = lax.broadcasted_iota(jnp.int32, (8, LANES), 1)

    def patch_step(p, _):
        y = [table[6 * p + 2 * c] for c in range(3)]
        total = (y[0] * y[0] + y[1] * y[1]) + y[2] * y[2]
        for c in range(3):
            work[p * 8 + c] = y[c]
            work[p * 8 + 4 + c] = table[6 * p + 2 * c + 1]
            sumacc[p * 8 + c] = jnp.zeros((8, LANES), f32)
        work[p * 8 + 3] = 1.0 + total * (1.0 / (4.0 * GAIN))
        return 0

    lax.fori_loop(0, PATCHES, patch_step, 0)

    for copy in copies:
        copy.wait()

    def block_step(block, _):
        start = block * LANES

        def point_step(group, held):
            first = group * 64
            ahead = lane - first
            held = list(held)
            for q in range(64):
                i = start + first + q
                x, y, z, square = data[0][0, i], data[1][0, i], data[2][0, i], data[6][0, i]
                ps = [names[s][0, i] * 8 for s in range(SLOTS)]
                term = []
                for s in range(SLOTS):
                    p = ps[s]
                    near = (work[p] * x + work[p + 1] * y) + (work[p + 2] * z + (work[p + 3] + square))
                    term.append(lax.rsqrt(near) * data[7 + s][0, i])
                old = [[sumacc[p + c] for c in range(3)] for p in ps]
                here = ahead == q
                for c in range(3):
                    dots = [work[ps[s] + 4 + c] * term[s] for s in range(SLOTS)]
                    value = (dots[0] + dots[1]) + (dots[2] + dots[3])
                    held[c] = jnp.where(here, jnp.sum(value, axis=1, keepdims=True), held[c])
                force = [data[3 + c][0, i] for c in range(3)]
                for s in range(SLOTS):
                    for c in range(3):
                        sumacc[ps[s] + c] = old[s][c] + term[s] * force[c]
            return tuple(held)

        held = lax.fori_loop(0, LANES // 64, point_step, (jnp.zeros((8, LANES), f32),) * 3)
        for c in range(3):
            total = jnp.sum(held[c], axis=0, keepdims=True)
            disp[pl.ds(c, 1), pl.ds(pl.multiple_of(start, LANES), LANES)] = total * (1.0 / 32.0)
        return 0

    lax.fori_loop(0, points // LANES, block_step, 0)

    def acc_step(p, _):
        for c in range(3):
            acc[3 * p + c] = sumacc[8 * p + c]
        return 0

    lax.fori_loop(0, PATCHES, acc_step, 0)


def fluid(patch, fields, table):
    points = fields.shape[2]
    return pl.pallas_call(
        fluid_kernel,
        out_shape=(
            jax.ShapeDtypeStruct((3, points), f32),
            jax.ShapeDtypeStruct((PATCHES * 3, 8, LANES), f32),
        ),
        in_specs=[pl.BlockSpec(memory_space=pl.ANY)] * 2 + [pl.BlockSpec(memory_space=VMEM)],
        out_specs=[pl.BlockSpec(memory_space=VMEM)] * 2,
        scratch_shapes=[
            VMEM((PATCHES * 8, 8, LANES), f32),
            VMEM((PATCHES * 8, 8, LANES), f32),
            pltpu.SemaphoreType.DMA((SLOTS + FIELDS,)),
        ]
        + [pltpu.SMEM((1, points), jnp.int32)] * SLOTS
        + [pltpu.SMEM((1, points), f32)] * FIELDS,
    )(patch, fields, table)


def local(node_coords, node_disp, node_list, factor, fluid_coords, fluid_loads, fluid_patch, blend_raw):
    table, fields, names = patch_tables(
        node_coords,
        node_disp,
        node_list,
        factor[0],
        fluid_coords,
        fluid_loads,
        blend_raw.T,
        fluid_patch.T,
    )
    fluid_disp, terms = fluid(names, fields, table.reshape(PATCHES * 6, 8, LANES))
    return fluid_disp, node_sums(terms.reshape(4, 4, 4, 2, 3, 8, LANES), node_list, factor[0])


def solution(mesh):
    placed = (
        P(None, "dev"),
        P(None, "dev"),
        P("dev", None),
        P("dev", None, None),
        P(None, "dev"),
        P(None, "dev"),
        P("dev", None),
        P("dev", None),
    )
    return jax.shard_map(
        local,
        mesh=mesh,
        in_specs=placed,
        out_specs=(P(None, "dev"), P(None, "dev")),
        check_vma=False,
    )
```

time: 236 us -> 152 us (0.64)
  Pallas kernels: 234 us -> 149 us
    pallas_call x1, Pallas kernels: 140 us -> 66.6 us  [fluid(): pl.pallas_call(fluid_kernel, out_shape=(jax.ShapeDtypeStruct((3, points),...]
    pallas_call x6 -> x2, Pallas kernels: 94.2 us -> 82.7 us  [the longest x1 45.8 us: patch_tables(): pl.pallas_call(patch_kernel, out_shape=(jax.ShapeDtypeStruct((4, 4, 4, 2,...]
where the time goes in v2:
time: 152 us; the launch traced here: 151 us
  Pallas kernels  149 us (98%)
    pallas_call x1, Pallas kernels, fluid(): pl.pallas_call(fluid_kernel, out_shape=(jax.ShapeDtypeStruct((3, points),...  66.6 us
    pallas_call x1, Pallas kernels, patch_tables(): pl.pallas_call(patch_kernel, out_shape=(jax.ShapeDtypeStruct((4, 4, 4, 2,...  45.8 us
    pallas_call x1, Pallas kernels, node_sums(): pl.pallas_call(load_kernel, out_shape=jax.ShapeDtypeStruct((3, NODE_DEV),...  36.9 us

profile of v2, /device:TPU:0, one launch (start us, length us, event | category | flops | bytes accessed | tf_op | source)
XLA Modules:
  0.0 151.2 jit_solution(7964946175065624945)
XLA Ops:
  0.6 45.8 %shard_map.95 = (f32[4,4,4,2,3,16,128]{6,5,4,3,2,1,0:T(8,128)}, f32[11,1,4096]{2,1,0:T(1,128)}, s32[4,1,4096]{2,1,0:T(1,128)}) custom-call(f32[3,512]{1,0:T(4,128)} %coords.1, f32[3,512]{1,0:T(4,128)} %disp.1, s32[1,1024]{1,0:T(1,128)} %ids.3, f32[1024,1024]{1,0:T(8,128)} %bitcast.5, f32[3,4096]{1,0:T(4,128)} %fluid_x.1, f32[3,4096]{1,0:T(4,128)} %fluid_f.1, ...), custom_call_target="tpu_custom_call" | custom-call | tf_op jit(solution)/shard_map/pallas_call | solution.py:264
  46.4 66.6 %shard_map.96 = (f32[3,4096]{1,0:T(4,128)}, f32[384,8,128]{2,1,0:T(8,128)}) custom-call(s32[4,1,4096]{2,1,0:T(1,128)} %get-tuple-element.7.refs_0_, f32[11,1,4096]{2,1,0:T(1,128)} %get-tuple-element.8.refs_1_, f32[768,8,128]{2,1,0:T(8,128)} %bitcast.7), custom_call_target="tpu_custom_call" | custom-call | tf_op jit(solution)/shard_map/pallas_call | solution.py:414
  113.0 36.9 %shard_map.97 = f32[3,512]{1,0:T(4,128)} custom-call(f32[4,4,4,2,3,8,128]{6,5,4,3,2,1,0:T(8,128)} %bitcast.8, s32[1,1024]{1,0:T(1,128)} %ids.3, f32[1024,1024]{1,0:T(8,128)} %bitcast.6), custom_call_target="tpu_custom_call" | custom-call | tf_op jit(solution)/shard_map/pallas_call | solution.py:323
  149.9 1.3 copy.11

commit v3 on v2

--- a/solution.py
+++ b/solution.py
@@ -56,31 +56,60 @@
     pass
 
 
-def gather_stages(out, place_now, sems, beside):
+def gather_stages(out, place_now, sems, beside, late=None):
     me, core, spot = place_now
     send_sem, recv_sem, core_send, core_recv = sems
+    partner = me + 1 - 2 * core
     for stage in range(3):
-        copies = []
-        for g in range(3):
+        copies, passed = [], []
+
+        def where(g, last):
             axis = (g + stage) % 3
             done = [(g + t) % 3 for t in range(stage)]
-            where = tuple(slice(None) if a in done else spot[a] for a in range(3)) + (core, g)
-            for step in (1, 2, 3):
-                part = out.at[where]
-                copies.append(
-                    send(
-                        part,
-                        part,
-                        send_sem.at[stage, g, step - 1],
-                        recv_sem.at[stage, g, 3 - step],
-                        peer_of(me, spot, axis, step),
+            spots = [slice(None) if a in done else spot[a] for a in range(3)]
+            spots[axis] = last
+            return tuple(spots) + (core, g)
+
+        def start(rows, turn):
+            for g in range(3):
+                axis = (g + stage) % 3
+                for step in (1, 2, 3):
+                    part = out.at[where(g, spot[axis]) + rows]
+                    copies.append(
+                        send(
+                            part,
+                            part,
+                            send_sem.at[turn, g, step - 1],
+                            recv_sem.at[turn, g, 3 - step],
+                            peer_of(me, spot, axis, step),
+                        )
                     )
-                )
+
+        if stage == 0 and late is not None:
+            start((pl.ds(8, 8),), 0)
+            late()
+            start((pl.ds(0, 8),), 3)
+        else:
+            start((), stage)
+        if stage < 2:
+            beside[stage]()
+            for copy in copies:
+                copy.wait()
+            continue
+        for g in range(3):
+            part = out.at[where(g, spot[(g + stage) % 3])]
+            passed.append(send(part, part, core_send.at[g, 0], core_recv.at[g, 0], partner))
         beside[stage]()
+        for k, step in enumerate((3, 1, 2)):
+            for g in range(3):
+                axis = (g + stage) % 3
+                copies[3 * g + step - 1].wait_recv()
+                part = out.at[where(g, lax.rem(spot[axis] + SIDE - step, SIDE))]
+                passed.append(send(part, part, core_send.at[g, 1 + k], core_recv.at[g, 1 + k], partner))
         for copy in copies:
+            copy.wait_send()
+        for copy in passed:
             copy.wait()
-    part = out.at[:, :, :, core]
-    send(part, part, core_send, core_recv, me + 1 - 2 * core).wait()
 
 
 def sum_stages(terms, place_now, buffers, sems):
@@ -142,8 +171,10 @@
     ]
 
 
-def stage_sems():
+def stage_sems(gather):
     dma = pltpu.SemaphoreType.DMA
+    if gather:
+        return [dma((4, 3, 3)), dma((4, 3, 3)), dma((3, 4)), dma((3, 4))]
     return [dma((3, 3, 3)), dma((3, 3, 3)), dma, dma]
 
 
@@ -248,14 +279,18 @@
 
     moved = jnp.concatenate(pick(1) + [jnp.zeros((5, PN), f32)], axis=0)
     coeffs = apply_inverse(moved, high, low)
-    centres = pick(0)
-    for g in range(3):
-        scaled = centres[g] * (-2.0 * GAIN)
-        for s in range(8):
-            lanes = slice(s * LANES, (s + 1) * LANES)
-            table[spot[0], spot[1], spot[2], core, g, pl.ds(s, 1), :] = scaled[:, lanes]
-            table[spot[0], spot[1], spot[2], core, g, pl.ds(8 + s, 1), :] = coeffs[g : g + 1, lanes]
-    gather_stages(table, (me, core, spot), table_sems, (nothing,) * 3)
+
+    def fill(values, first):
+        for g in range(3):
+            for s in range(8):
+                lanes = slice(s * LANES, (s + 1) * LANES)
+                table[spot[0], spot[1], spot[2], core, g, pl.ds(first + s, 1), :] = values[g][:, lanes]
+
+    def fill_centres():
+        fill([y * (-2.0 * GAIN) for y in pick(0)], 0)
+
+    fill([coeffs[g : g + 1] for g in range(3)], 8)
+    gather_stages(table, (me, core, spot), table_sems, (nothing,) * 3, fill_centres)
 
 
 def patch_tables(node_coords, node_disp, node_list, factor, coords, loads, blend, names):
@@ -272,24 +307,27 @@
         out_specs=[vmem] * 3,
         scratch_shapes=[VMEM((4, 4, 4, 2, 3, 8, LANES), f32)]
         + factor_scratch()
-        + stage_sems()
-        + stage_sems(),
+        + stage_sems(True)
+        + stage_sems(True),
         compiler_params=pltpu.CompilerParams(
             collective_id=0, has_side_effects=True, vmem_limit_bytes=60 * 2**20
         ),
     )(node_coords, node_disp, node_list, factor, coords, loads, blend, names)
 
 
-def load_kernel(terms, ids, factor_hbm, out, spread, factor, high, low, marks, factor_sem, *rest):
+def load_kernel(terms_hbm, ids, factor_hbm, out, spread, factor, high, low, marks, factor_sem, terms, terms_sem, *rest):
     patch_buffers, node_buffers = rest[:7], rest[7:14]
     patch_sems, node_sems = rest[14:18], rest[18:22]
     me, core, spot = place()
     load = pltpu.make_async_copy(factor_hbm, factor, factor_sem)
+    fill = pltpu.make_async_copy(terms_hbm, terms, terms_sem)
+    fill.start()
     load.start()
     barrier = greet(me, core, spot)
     mark_local(ids, marks)
     load.wait()
     split_factor(factor, high, low)
+    fill.wait()
     pl.semaphore_wait(barrier, 10)
     summed = sum_stages(terms, (me, core, spot), patch_buffers, patch_sems)
     rows = [jnp.concatenate([part[s : s + 1] for s in range(8)], axis=1) for part in summed]
@@ -320,17 +358,19 @@
 
 def node_sums(terms, node_list, factor):
     vmem = pl.BlockSpec(memory_space=VMEM)
+    hbm = pl.BlockSpec(memory_space=pl.ANY)
     return pl.pallas_call(
         load_kernel,
         out_shape=jax.ShapeDtypeStruct((3, NODE_DEV), f32),
-        in_specs=[vmem] * 2 + [pl.BlockSpec(memory_space=pl.ANY)],
+        in_specs=[hbm, vmem, hbm],
         out_specs=vmem,
         scratch_shapes=[VMEM((4, 4, 4, 2, 3, 4, LANES), f32)]
         + factor_scratch()
+        + [VMEM((4, 4, 4, 2, 3, 8, LANES), f32), pltpu.SemaphoreType.DMA]
         + sum_buffers(8)
         + sum_buffers(4)
-        + stage_sems()
-        + stage_sems(),
+        + stage_sems(False)
+        + stage_sems(False),
         compiler_params=pltpu.CompilerParams(
             collective_id=1, has_side_effects=True, vmem_limit_bytes=60 * 2**20
         ),
@@ -341,8 +381,10 @@
 
 
 def fluid_kernel(*refs):
-    patch, fields, table, disp, acc, work, sumacc, got = refs[:8]
-    names, data = refs[8 : 8 + SLOTS], refs[8 + SLOTS :]
+    patch, fields, table_hbm, disp, acc, work, table, table_sem, got = refs[:9]
+    names, data = refs[9 : 9 + SLOTS], refs[9 + SLOTS :]
+    fill = pltpu.make_async_copy(table_hbm, table, table_sem)
+    fill.start()
     copies = [pltpu.make_async_copy(patch.at[s], names[s], got.at[s]) for s in range(SLOTS)]
     copies += [pltpu.make_async_copy(fields.at[j], data[j], got.at[SLOTS + j]) for j in range(FIELDS)]
     for copy in copies:
@@ -356,10 +398,11 @@
         for c in range(3):
             work[p * 8 + c] = y[c]
             work[p * 8 + 4 + c] = table[6 * p + 2 * c + 1]
-            sumacc[p * 8 + c] = jnp.zeros((8, LANES), f32)
+            acc[p * 3 + c] = jnp.zeros((8, LANES), f32)
         work[p * 8 + 3] = 1.0 + total * (1.0 / (4.0 * GAIN))
         return 0
 
+    fill.wait()
     lax.fori_loop(0, PATCHES, patch_step, 0)
 
     for copy in copies:
@@ -375,22 +418,22 @@
             for q in range(64):
                 i = start + first + q
                 x, y, z, square = data[0][0, i], data[1][0, i], data[2][0, i], data[6][0, i]
-                ps = [names[s][0, i] * 8 for s in range(SLOTS)]
+                ps = [names[s][0, i] for s in range(SLOTS)]
                 term = []
                 for s in range(SLOTS):
-                    p = ps[s]
+                    p = ps[s] * 8
                     near = (work[p] * x + work[p + 1] * y) + (work[p + 2] * z + (work[p + 3] + square))
                     term.append(lax.rsqrt(near) * data[7 + s][0, i])
-                old = [[sumacc[p + c] for c in range(3)] for p in ps]
+                old = [[acc[p * 3 + c] for c in range(3)] for p in ps]
                 here = ahead == q
                 for c in range(3):
-                    dots = [work[ps[s] + 4 + c] * term[s] for s in range(SLOTS)]
+                    dots = [work[ps[s] * 8 + 4 + c] * term[s] for s in range(SLOTS)]
                     value = (dots[0] + dots[1]) + (dots[2] + dots[3])
                     held[c] = jnp.where(here, jnp.sum(value, axis=1, keepdims=True), held[c])
                 force = [data[3 + c][0, i] for c in range(3)]
                 for s in range(SLOTS):
                     for c in range(3):
-                        sumacc[ps[s] + c] = old[s][c] + term[s] * force[c]
+                        acc[ps[s] * 3 + c] = old[s][c] + term[s] * force[c]
             return tuple(held)
 
         held = lax.fori_loop(0, LANES // 64, point_step, (jnp.zeros((8, LANES), f32),) * 3)
@@ -400,13 +443,6 @@
         return 0
 
     lax.fori_loop(0, points // LANES, block_step, 0)
-
-    def acc_step(p, _):
-        for c in range(3):
-            acc[3 * p + c] = sumacc[8 * p + c]
-        return 0
-
-    lax.fori_loop(0, PATCHES, acc_step, 0)
 
 
 def fluid(patch, fields, table):
@@ -417,11 +453,12 @@
             jax.ShapeDtypeStruct((3, points), f32),
             jax.ShapeDtypeStruct((PATCHES * 3, 8, LANES), f32),
         ),
-        in_specs=[pl.BlockSpec(memory_space=pl.ANY)] * 2 + [pl.BlockSpec(memory_space=VMEM)],
+        in_specs=[pl.BlockSpec(memory_space=pl.ANY)] * 3,
         out_specs=[pl.BlockSpec(memory_space=VMEM)] * 2,
         scratch_shapes=[
             VMEM((PATCHES * 8, 8, LANES), f32),
-            VMEM((PATCHES * 8, 8, LANES), f32),
+            VMEM((PATCHES * 6, 8, LANES), f32),
+            pltpu.SemaphoreType.DMA,
             pltpu.SemaphoreType.DMA((SLOTS + FIELDS,)),
         ]
         + [pltpu.SMEM((1, points), jnp.int32)] * SLOTS

time: 152 us -> 149 us (0.980)
  Pallas kernels: 149 us -> 147 us
    pallas_call x1, Pallas kernels: 45.8 us -> 44.2 us  [patch_tables(): pl.pallas_call(patch_kernel, out_shape=(jax.ShapeDtypeStruct((4, 4, 4, 2,...]
where the time goes in v3:
time: 149 us
  Pallas kernels  147 us (99%)
    pallas_call x1, Pallas kernels, fluid(): pl.pallas_call(fluid_kernel, out_shape=(jax.ShapeDtypeStruct((3, points),...  65.2 us
    pallas_call x1, Pallas kernels, patch_tables(): pl.pallas_call(patch_kernel, out_shape=(jax.ShapeDtypeStruct((4, 4, 4, 2,...  44.2 us
    pallas_call x1, Pallas kernels, node_sums(): pl.pallas_call(load_kernel, out_shape=jax.ShapeDtypeStruct((3, NODE_DEV),...  37.2 us

profile of v3, /device:TPU:0, one launch (start us, length us, event | category | flops | bytes accessed | tf_op | source)
XLA Modules:
  0.0 148.6 jit_solution(8874832926700030464)
XLA Ops:
  0.6 44.2 %shard_map.95 = (f32[4,4,4,2,3,16,128]{6,5,4,3,2,1,0:T(8,128)}, f32[11,1,4096]{2,1,0:T(1,128)}, s32[4,1,4096]{2,1,0:T(1,128)}) custom-call(f32[3,512]{1,0:T(4,128)} %coords.1, f32[3,512]{1,0:T(4,128)} %disp.1, s32[1,1024]{1,0:T(1,128)} %ids.3, f32[1024,1024]{1,0:T(8,128)} %bitcast.5, f32[3,4096]{1,0:T(4,128)} %fluid_x.1, f32[3,4096]{1,0:T(4,128)} %fluid_f.1, ...), custom_call_target="tpu_custom_call" | custom-call | tf_op jit(solution)/shard_map/pallas_call | solution.py:299
  44.9 65.2 %shard_map.96 = (f32[3,4096]{1,0:T(4,128)}, f32[384,8,128]{2,1,0:T(8,128)}) custom-call(s32[4,1,4096]{2,1,0:T(1,128)} %get-tuple-element.7.refs_0_, f32[11,1,4096]{2,1,0:T(1,128)} %get-tuple-element.8.refs_1_, f32[768,8,128]{2,1,0:T(8,128)} %bitcast.7), custom_call_target="tpu_custom_call" | custom-call | tf_op jit(solution)/shard_map/pallas_call | solution.py:450
  110.0 37.2 %shard_map.97 = f32[3,512]{1,0:T(4,128)} custom-call(f32[4,4,4,2,3,8,128]{6,5,4,3,2,1,0:T(8,128)} %bitcast.8, s32[1,1024]{1,0:T(1,128)} %ids.3, f32[1024,1024]{1,0:T(8,128)} %bitcast.6), custom_call_target="tpu_custom_call" | custom-call | tf_op jit(solution)/shard_map/pallas_call | solution.py:362
  147.3 1.3 copy.11

commit v4 on v3

--- a/solution.py
+++ b/solution.py
@@ -29,13 +29,28 @@
     return me + (lax.rem(spot[axis] + step, SIDE) - spot[axis]) * STRIDE[axis]
 
 
-def greet(me, core, spot):
+def plane_peers(me, spot, axes):
+    steps = [(a, b) for a in range(SIDE) for b in range(SIDE) if a or b]
+    steps.sort(key=lambda ab: min(ab[0], SIDE - ab[0]) + min(ab[1], SIDE - ab[1]))
+    out = []
+    for a, b in steps:
+        device = peer_of(peer_of(me, spot, axes[0], a), spot, axes[1], b)
+        out.append((device, (a, b), ((SIDE - a) % SIDE) * SIDE + (SIDE - b) % SIDE))
+    return out
+
+
+LINES = 3 * 3 + 1
+PLANES = 3 * 3 + 3 * 9 + 1
+
+
+def greet(me, core, spot, planes):
     barrier = pltpu.get_barrier_semaphore()
-    for axis in range(3):
-        for step in (1, 2, 3):
-            peer = peer_of(me, spot, axis, step)
-            pl.semaphore_signal(barrier, inc=1, device_id=(peer,), device_id_type=MESH)
-    pl.semaphore_signal(barrier, inc=1, device_id=(me + 1 - 2 * core,), device_id_type=MESH)
+    peers = [me + 1 - 2 * core]
+    for g in range(3):
+        near = plane_peers(me, spot, (g, (g + 1) % 3))
+        peers += [d for d, (a, b), _ in near if a and (planes or not b)]
+    for peer in peers:
+        pl.semaphore_signal(barrier, inc=1, device_id=(peer,), device_id_type=MESH)
     return barrier
 
 
@@ -114,47 +129,57 @@
 
 def sum_stages(terms, place_now, buffers, sems):
     me, core, spot = place_now
-    core_in, s1, r2, s2, r3, s3, r4 = buffers
-    send_sem, recv_sem, core_send, core_recv = sems
+    core_in, s1, r2, s2, r3 = buffers
+    plane_send, plane_recv, line_send, line_recv, core_send, core_recv = sems
     part = terms.at[:, :, :, 1 - core]
     send(part, core_in, core_send, core_recv, me + 1 - 2 * core).wait()
     for a in range(SIDE):
         for g in range(3):
             s1[g, a] = terms[a, :, :, core, g] + core_in[a, :, :, g]
-    sums, landed = (s1, s2, s3), (r2, r3, r4)
+    copies = []
+    for g in range(3):
+        for step in (1, 2, 3):
+            to = lax.rem(spot[g] + step, SIDE)
+            copies.append(
+                send(
+                    s1.at[(g,) + (slice(None),) * g + (to,)],
+                    r2.at[g, 3 - step],
+                    line_send.at[g, step - 1],
+                    line_recv.at[g, 3 - step],
+                    peer_of(me, spot, g, step),
+                )
+            )
+    for g in range(3):
+        for k in range(3):
+            copies[3 * g + k].wait_recv()
+        mine = (g,) + (slice(None),) * g + (spot[g],)
+        s2[g] = (s1[mine] + r2[g, 0]) + (r2[g, 1] + r2[g, 2])
+    left = [[a for a in range(3) if a != g] for g in range(3)]
+    around = [plane_peers(me, spot, left[g]) for g in range(3)]
+    spread = [[], [], []]
+    for k in range(15):
+        for g in range(3):
+            device, (a, b), there = around[g][k]
+            to = (lax.rem(spot[left[g][0]] + a, SIDE), lax.rem(spot[left[g][1]] + b, SIDE))
+            spread[g].append(
+                send(
+                    s2.at[(g,) + to],
+                    r3.at[g, there],
+                    plane_send.at[g, SIDE * a + b],
+                    plane_recv.at[g, there],
+                    device,
+                )
+            )
     totals = []
-    for stage in range(3):
-        src, dst = sums[stage], landed[stage]
-        ahead = []
-        for g in range(3):
-            gone = [(g + t) % 3 for t in range(stage)]
-            ahead.append([a for a in range(3) if a not in gone].index((g + stage) % 3))
-        copies = []
-        for g in range(3):
-            axis = (g + stage) % 3
-            for step in (1, 2, 3):
-                to = lax.rem(spot[axis] + step, SIDE)
-                copies.append(
-                    send(
-                        src.at[(g,) + (slice(None),) * ahead[g] + (to,)],
-                        dst.at[g, 3 - step],
-                        send_sem.at[stage, g, step - 1],
-                        recv_sem.at[stage, g, 3 - step],
-                        peer_of(me, spot, axis, step),
-                    )
-                )
-        for g in range(3):
-            axis = (g + stage) % 3
-            for k in range(3):
-                copies[3 * g + k].wait_recv()
-            mine = (g,) + (slice(None),) * ahead[g] + (spot[axis],)
-            total = (src[mine] + dst[g, 0]) + (dst[g, 1] + dst[g, 2])
-            if stage < 2:
-                sums[stage + 1][g] = total
-            else:
-                totals.append(total)
-        for copy in copies:
-            copy.wait_send()
+    for g in range(3):
+        for copy in spread[g]:
+            copy.wait_recv()
+        terms_now = [s2[g, spot[left[g][0]], spot[left[g][1]]]] + [r3[g, k] for k in range(1, 16)]
+        while len(terms_now) > 1:
+            terms_now = [x + y for x, y in zip(terms_now[::2], terms_now[1::2])]
+        totals.append(terms_now[0])
+    for copy in copies + spread[0] + spread[1] + spread[2]:
+        copy.wait_send()
     return totals
 
 
@@ -165,9 +190,7 @@
         VMEM((3, 4, 4, 4) + tail, f32),
         VMEM((3, 3, 4, 4) + tail, f32),
         VMEM((3, 4, 4) + tail, f32),
-        VMEM((3, 3, 4) + tail, f32),
-        VMEM((3, 4) + tail, f32),
-        VMEM((3, 3) + tail, f32),
+        VMEM((3, 16) + tail, f32),
     ]
 
 
@@ -175,7 +198,7 @@
     dma = pltpu.SemaphoreType.DMA
     if gather:
         return [dma((4, 3, 3)), dma((4, 3, 3)), dma((3, 4)), dma((3, 4))]
-    return [dma((3, 3, 3)), dma((3, 3, 3)), dma, dma]
+    return [dma((3, 16)), dma((3, 16)), dma((3, 3)), dma((3, 3)), dma, dma]
 
 
 def halves(x):
@@ -232,14 +255,14 @@
     me, core, spot = place()
     load = pltpu.make_async_copy(factor_hbm, factor, factor_sem)
     load.start()
-    barrier = greet(me, core, spot)
+    barrier = greet(me, core, spot, False)
     for g in range(3):
         for r in range(4):
             lanes = pl.ds(r * LANES, LANES)
             nodes[spot[0], spot[1], spot[2], core, g, pl.ds(r, 1), :] = coords[pl.ds(g, 1), lanes]
             nodes[spot[0], spot[1], spot[2], core, g, pl.ds(4 + r, 1), :] = disp[pl.ds(g, 1), lanes]
     mark_local(ids, marks)
-    pl.semaphore_wait(barrier, 10)
+    pl.semaphore_wait(barrier, LINES)
 
     def fill_fields():
         x, f, b = fluid_x[...], fluid_f[...], blend[...]
@@ -316,19 +339,19 @@
 
 
 def load_kernel(terms_hbm, ids, factor_hbm, out, spread, factor, high, low, marks, factor_sem, terms, terms_sem, *rest):
-    patch_buffers, node_buffers = rest[:7], rest[7:14]
-    patch_sems, node_sems = rest[14:18], rest[18:22]
+    patch_buffers, node_buffers = rest[:5], rest[5:10]
+    patch_sems, node_sems = rest[10:16], rest[16:22]
     me, core, spot = place()
     load = pltpu.make_async_copy(factor_hbm, factor, factor_sem)
     fill = pltpu.make_async_copy(terms_hbm, terms, terms_sem)
     fill.start()
     load.start()
-    barrier = greet(me, core, spot)
+    barrier = greet(me, core, spot, True)
     mark_local(ids, marks)
     load.wait()
     split_factor(factor, high, low)
     fill.wait()
-    pl.semaphore_wait(barrier, 10)
+    pl.semaphore_wait(barrier, PLANES)
     summed = sum_stages(terms, (me, core, spot), patch_buffers, patch_sems)
     rows = [jnp.concatenate([part[s : s + 1] for s in range(8)], axis=1) for part in summed]
     rows = jnp.concatenate(rows + [jnp.zeros((5, PN), f32)], axis=0)
@@ -378,6 +401,7 @@
 
 
 FIELDS = 11
+EARLY = 4
 
 
 def fluid_kernel(*refs):
@@ -385,11 +409,21 @@
     names, data = refs[9 : 9 + SLOTS], refs[9 + SLOTS :]
     fill = pltpu.make_async_copy(table_hbm, table, table_sem)
     fill.start()
-    copies = [pltpu.make_async_copy(patch.at[s], names[s], got.at[s]) for s in range(SLOTS)]
-    copies += [pltpu.make_async_copy(fields.at[j], data[j], got.at[SLOTS + j]) for j in range(FIELDS)]
-    for copy in copies:
-        copy.start()
     points = disp.shape[1]
+    rows = [(patch.at[s], names[s]) for s in range(SLOTS)]
+    rows += [(fields.at[j], data[j]) for j in range(FIELDS)]
+
+    def scalars(k):
+        first = EARLY * LANES
+        where = (slice(None), pl.ds(first, points - first) if k else pl.ds(0, first))
+        return [
+            pltpu.make_async_copy(src.at[where], dst.at[where], got.at[k, j])
+            for j, (src, dst) in enumerate(rows)
+        ]
+
+    for k in range(2):
+        for copy in scalars(k):
+            copy.start()
     lane = lax.broadcasted_iota(jnp.int32, (8, LANES), 1)
 
     def patch_step(p, _):
@@ -405,17 +439,22 @@
     fill.wait()
     lax.fori_loop(0, PATCHES, patch_step, 0)
 
-    for copy in copies:
+    for copy in scalars(0):
         copy.wait()
 
     def block_step(block, _):
         start = block * LANES
 
+        @pl.when(block == EARLY)
+        def _():
+            for copy in scalars(1):
+                copy.wait()
+
         def point_step(group, held):
-            first = group * 64
+            first = group * 128
             ahead = lane - first
             held = list(held)
-            for q in range(64):
+            for q in range(128):
                 i = start + first + q
                 x, y, z, square = data[0][0, i], data[1][0, i], data[2][0, i], data[6][0, i]
                 ps = [names[s][0, i] for s in range(SLOTS)]
@@ -436,7 +475,7 @@
                         acc[ps[s] * 3 + c] = old[s][c] + term[s] * force[c]
             return tuple(held)
 
-        held = lax.fori_loop(0, LANES // 64, point_step, (jnp.zeros((8, LANES), f32),) * 3)
+        held = lax.fori_loop(0, LANES // 128, point_step, (jnp.zeros((8, LANES), f32),) * 3)
         for c in range(3):
             total = jnp.sum(held[c], axis=0, keepdims=True)
             disp[pl.ds(c, 1), pl.ds(pl.multiple_of(start, LANES), LANES)] = total * (1.0 / 32.0)
@@ -459,7 +498,7 @@
             VMEM((PATCHES * 8, 8, LANES), f32),
             VMEM((PATCHES * 6, 8, LANES), f32),
             pltpu.SemaphoreType.DMA,
-            pltpu.SemaphoreType.DMA((SLOTS + FIELDS,)),
+            pltpu.SemaphoreType.DMA((2, SLOTS + FIELDS)),
         ]
         + [pltpu.SMEM((1, points), jnp.int32)] * SLOTS
         + [pltpu.SMEM((1, points), f32)] * FIELDS,

time: 149 us -> 143 us (0.960)
  Pallas kernels: 147 us -> 141 us
    pallas_call x1, Pallas kernels: 65.2 us -> 62 us  [fluid(): pl.pallas_call(fluid_kernel, out_shape=(jax.ShapeDtypeStruct((3, points),...]
    pallas_call x1, Pallas kernels: 37.2 us -> 34.6 us  [node_sums(): pl.pallas_call(load_kernel, out_shape=jax.ShapeDtypeStruct((3, NODE_DEV),...]
where the time goes in v4:
time: 143 us
  Pallas kernels  141 us (99%)
    pallas_call x1, Pallas kernels, fluid(): pl.pallas_call(fluid_kernel, out_shape=(jax.ShapeDtypeStruct((3, points),...  62 us
    pallas_call x1, Pallas kernels, patch_tables(): pl.pallas_call(patch_kernel, out_shape=(jax.ShapeDtypeStruct((4, 4, 4, 2,...  44.2 us
    pallas_call x1, Pallas kernels, node_sums(): pl.pallas_call(load_kernel, out_shape=jax.ShapeDtypeStruct((3, NODE_DEV),...  34.6 us

profile of v4, /device:TPU:0, one launch (start us, length us, event | category | flops | bytes accessed | tf_op | source)
XLA Modules:
  0.0 142.8 jit_solution(12055276775796900943)
XLA Ops:
  0.6 44.2 %shard_map.95 = (f32[4,4,4,2,3,16,128]{6,5,4,3,2,1,0:T(8,128)}, f32[11,1,4096]{2,1,0:T(1,128)}, s32[4,1,4096]{2,1,0:T(1,128)}) custom-call(f32[3,512]{1,0:T(4,128)} %coords.1, f32[3,512]{1,0:T(4,128)} %disp.1, s32[1,1024]{1,0:T(1,128)} %ids.3, f32[1024,1024]{1,0:T(8,128)} %bitcast.5, f32[3,4096]{1,0:T(4,128)} %fluid_x.1, f32[3,4096]{1,0:T(4,128)} %fluid_f.1, ...), custom_call_target="tpu_custom_call" | custom-call | tf_op jit(solution)/shard_map/pallas_call | solution.py:322
  44.9 62.0 %shard_map.96 = (f32[3,4096]{1,0:T(4,128)}, f32[384,8,128]{2,1,0:T(8,128)}) custom-call(s32[4,1,4096]{2,1,0:T(1,128)} %get-tuple-element.7.refs_0_, f32[11,1,4096]{2,1,0:T(1,128)} %get-tuple-element.8.refs_1_, f32[768,8,128]{2,1,0:T(8,128)} %bitcast.7), custom_call_target="tpu_custom_call" | custom-call | tf_op jit(solution)/shard_map/pallas_call | solution.py:489
  106.9 34.6 %shard_map.97 = f32[3,512]{1,0:T(4,128)} custom-call(f32[4,4,4,2,3,8,128]{6,5,4,3,2,1,0:T(8,128)} %bitcast.8, s32[1,1024]{1,0:T(1,128)} %ids.3, f32[1024,1024]{1,0:T(8,128)} %bitcast.6), custom_call_target="tpu_custom_call" | custom-call | tf_op jit(solution)/shard_map/pallas_call | solution.py:385
  141.5 1.3 copy.11

commit v5 on v4

--- a/solution.py
+++ b/solution.py
@@ -75,69 +75,71 @@
     me, core, spot = place_now
     send_sem, recv_sem, core_send, core_recv = sems
     partner = me + 1 - 2 * core
-    for stage in range(3):
-        copies, passed = [], []
-
-        def where(g, last):
-            axis = (g + stage) % 3
-            done = [(g + t) % 3 for t in range(stage)]
-            spots = [slice(None) if a in done else spot[a] for a in range(3)]
-            spots[axis] = last
-            return tuple(spots) + (core, g)
-
-        def start(rows, turn):
-            for g in range(3):
-                axis = (g + stage) % 3
-                for step in (1, 2, 3):
-                    part = out.at[where(g, spot[axis]) + rows]
-                    copies.append(
-                        send(
-                            part,
-                            part,
-                            send_sem.at[turn, g, step - 1],
-                            recv_sem.at[turn, g, 3 - step],
-                            peer_of(me, spot, axis, step),
-                        )
-                    )
-
-        if stage == 0 and late is not None:
-            start((pl.ds(8, 8),), 0)
-            late()
-            start((pl.ds(0, 8),), 3)
-        else:
-            start((), stage)
-        if stage < 2:
-            beside[stage]()
-            for copy in copies:
+
+    def where(stage, g, last):
+        done = [(g + t) % 3 for t in range(stage)]
+        spots = [slice(None) if a in done else spot[a] for a in range(3)]
+        spots[(g + stage) % 3] = last
+        return tuple(spots) + (core, g)
+
+    def start(stage, g, rows, turn):
+        axis = (g + stage) % 3
+        part = out.at[where(stage, g, spot[axis]) + rows]
+        return [
+            send(
+                part,
+                part,
+                send_sem.at[turn, g, step - 1],
+                recv_sem.at[turn, g, 3 - step],
+                peer_of(me, spot, axis, step),
+            )
+            for step in (1, 2, 3)
+        ]
+
+    if late is not None:
+        copies = [start(0, g, (pl.ds(8, 8),), 0) for g in range(3)]
+        late()
+        copies = [copies[g] + start(0, g, (pl.ds(0, 8),), 3) for g in range(3)]
+    else:
+        copies = [start(0, g, (), 0) for g in range(3)]
+    beside[0]()
+    passed = []
+    for stage in (1, 2):
+        ahead = []
+        for g in range(3):
+            for copy in copies[g]:
                 copy.wait()
-            continue
+            ahead.append(start(stage, g, (), stage))
+            if stage == 2:
+                part = out.at[where(stage, g, spot[(g + stage) % 3])]
+                passed.append(send(part, part, core_send.at[g, 0], core_recv.at[g, 0], partner))
+        copies = ahead
+        beside[stage]()
+    for k, step in enumerate((3, 1, 2)):
         for g in range(3):
-            part = out.at[where(g, spot[(g + stage) % 3])]
-            passed.append(send(part, part, core_send.at[g, 0], core_recv.at[g, 0], partner))
-        beside[stage]()
-        for k, step in enumerate((3, 1, 2)):
-            for g in range(3):
-                axis = (g + stage) % 3
-                copies[3 * g + step - 1].wait_recv()
-                part = out.at[where(g, lax.rem(spot[axis] + SIDE - step, SIDE))]
-                passed.append(send(part, part, core_send.at[g, 1 + k], core_recv.at[g, 1 + k], partner))
-        for copy in copies:
-            copy.wait_send()
-        for copy in passed:
-            copy.wait()
+            axis = (g + 2) % 3
+            copies[g][step - 1].wait_recv()
+            part = out.at[where(2, g, lax.rem(spot[axis] + SIDE - step, SIDE))]
+            passed.append(send(part, part, core_send.at[g, 1 + k], core_recv.at[g, 1 + k], partner))
+    for copy in copies[0] + copies[1] + copies[2]:
+        copy.wait_send()
+    for copy in passed:
+        copy.wait()
 
 
 def sum_stages(terms, place_now, buffers, sems):
     me, core, spot = place_now
     core_in, s1, r2, s2, r3 = buffers
     plane_send, plane_recv, line_send, line_recv, core_send, core_recv = sems
-    part = terms.at[:, :, :, 1 - core]
-    send(part, core_in, core_send, core_recv, me + 1 - 2 * core).wait()
-    for a in range(SIDE):
-        for g in range(3):
-            s1[g, a] = terms[a, :, :, core, g] + core_in[a, :, :, g]
+    swaps = []
+    for g in range(3):
+        part = terms.at[:, :, :, 1 - core, g]
+        swaps.append(send(part, core_in.at[g], core_send.at[g], core_recv.at[g], me + 1 - 2 * core))
     copies = []
     for g in range(3):
+        swaps[g].wait_recv()
+        for a in range(SIDE):
+            s1[g, a] = terms[a, :, :, core, g] + core_in[g, a]
         for step in (1, 2, 3):
             to = lax.rem(spot[g] + step, SIDE)
             copies.append(
@@ -149,17 +151,14 @@
                     peer_of(me, spot, g, step),
                 )
             )
+    spread = [[], [], []]
+    left = [[a for a in range(3) if a != g] for g in range(3)]
     for g in range(3):
         for k in range(3):
             copies[3 * g + k].wait_recv()
         mine = (g,) + (slice(None),) * g + (spot[g],)
         s2[g] = (s1[mine] + r2[g, 0]) + (r2[g, 1] + r2[g, 2])
-    left = [[a for a in range(3) if a != g] for g in range(3)]
-    around = [plane_peers(me, spot, left[g]) for g in range(3)]
-    spread = [[], [], []]
-    for k in range(15):
-        for g in range(3):
-            device, (a, b), there = around[g][k]
+        for device, (a, b), there in plane_peers(me, spot, left[g]):
             to = (lax.rem(spot[left[g][0]] + a, SIDE), lax.rem(spot[left[g][1]] + b, SIDE))
             spread[g].append(
                 send(
@@ -178,7 +177,7 @@
         while len(terms_now) > 1:
             terms_now = [x + y for x, y in zip(terms_now[::2], terms_now[1::2])]
         totals.append(terms_now[0])
-    for copy in copies + spread[0] + spread[1] + spread[2]:
+    for copy in swaps + copies + spread[0] + spread[1] + spread[2]:
         copy.wait_send()
     return totals
 
@@ -186,7 +185,7 @@
 def sum_buffers(rows):
     tail = (rows, LANES)
     return [
-        VMEM((4, 4, 4, 3) + tail, f32),
+        VMEM((3, 4, 4, 4) + tail, f32),
         VMEM((3, 4, 4, 4) + tail, f32),
         VMEM((3, 3, 4, 4) + tail, f32),
         VMEM((3, 4, 4) + tail, f32),
@@ -198,7 +197,7 @@
     dma = pltpu.SemaphoreType.DMA
     if gather:
         return [dma((4, 3, 3)), dma((4, 3, 3)), dma((3, 4)), dma((3, 4))]
-    return [dma((3, 16)), dma((3, 16)), dma((3, 3)), dma((3, 3)), dma, dma]
+    return [dma((3, 16)), dma((3, 16)), dma((3, 3)), dma((3, 3)), dma((3,)), dma((3,))]
 
 
 def halves(x):
@@ -355,7 +354,7 @@
     summed = sum_stages(terms, (me, core, spot), patch_buffers, patch_sems)
     rows = [jnp.concatenate([part[s : s + 1] for s in range(8)], axis=1) for part in summed]
     rows = jnp.concatenate(rows + [jnp.zeros((5, PN), f32)], axis=0)
-    loads = apply_inverse(rows * (1.0 / 32.0), high, low)
+    loads = apply_inverse(rows, high, low)
     where = at_owner(ids)
     parts = []
     for g in range(3):
@@ -517,7 +516,8 @@
         fluid_patch.T,
     )
     fluid_disp, terms = fluid(names, fields, table.reshape(PATCHES * 6, 8, LANES))
-    return fluid_disp, node_sums(terms.reshape(4, 4, 4, 2, 3, 8, LANES), node_list, factor[0])
+    node_loads = node_sums(terms.reshape(4, 4, 4, 2, 3, 8, LANES), node_list, factor[0])
+    return fluid_disp, node_loads * (1.0 / 32.0)
 
 
 def solution(mesh):

time: 143 us -> 142 us (level)
  Pallas kernels: 141 us -> 139 us
    pallas_call x1, Pallas kernels: 34.6 us -> 31.9 us  [node_sums(): pl.pallas_call(load_kernel, out_shape=jax.ShapeDtypeStruct((3, NODE_DEV),...]
where the time goes in v5:
time: 142 us; the launch traced here: 141 us
  Pallas kernels  139 us (98%)
    pallas_call x1, Pallas kernels, fluid(): pl.pallas_call(fluid_kernel, out_shape=(jax.ShapeDtypeStruct((3, points),...  62.1 us
    pallas_call x1, Pallas kernels, patch_tables(): pl.pallas_call(patch_kernel, out_shape=(jax.ShapeDtypeStruct((4, 4, 4, 2,...  44.9 us
    pallas_call x1, Pallas kernels, node_sums(): pl.pallas_call(load_kernel, out_shape=jax.ShapeDtypeStruct((3, NODE_DEV),...  31.9 us

profile of v5, /device:TPU:0, one launch (start us, length us, event | category | flops | bytes accessed | tf_op | source)
XLA Modules:
  0.0 140.8 jit_solution(1900546796066165145)
XLA Ops:
  0.6 44.9 %shard_map.95 = (f32[4,4,4,2,3,16,128]{6,5,4,3,2,1,0:T(8,128)}, f32[11,1,4096]{2,1,0:T(1,128)}, s32[4,1,4096]{2,1,0:T(1,128)}) custom-call(f32[3,512]{1,0:T(4,128)} %coords.1, f32[3,512]{1,0:T(4,128)} %disp.1, s32[1,1024]{1,0:T(1,128)} %ids.3, f32[1024,1024]{1,0:T(8,128)} %bitcast.5, f32[3,4096]{1,0:T(4,128)} %fluid_x.1, f32[3,4096]{1,0:T(4,128)} %fluid_f.1, ...), custom_call_target="tpu_custom_call" | custom-call | tf_op jit(solution)/shard_map/pallas_call | solution.py:321
  45.5 62.1 %shard_map.96 = (f32[3,4096]{1,0:T(4,128)}, f32[384,8,128]{2,1,0:T(8,128)}) custom-call(s32[4,1,4096]{2,1,0:T(1,128)} %get-tuple-element.7.refs_0_, f32[11,1,4096]{2,1,0:T(1,128)} %get-tuple-element.8.refs_1_, f32[768,8,128]{2,1,0:T(8,128)} %bitcast.7), custom_call_target="tpu_custom_call" | custom-call | tf_op jit(solution)/shard_map/pallas_call | solution.py:488
  107.6 31.9 %shard_map.97 = f32[3,512]{1,0:T(4,128)} custom-call(f32[4,4,4,2,3,8,128]{6,5,4,3,2,1,0:T(8,128)} %bitcast.8, s32[1,1024]{1,0:T(1,128)} %ids.3, f32[1024,1024]{1,0:T(8,128)} %bitcast.6), custom_call_target="tpu_custom_call" | custom-call | tf_op jit(solution)/shard_map/pallas_call | solution.py:384
  139.5 1.3 broadcast_multiply_fusion

commit v6 on v5

--- a/solution.py
+++ b/solution.py
@@ -404,8 +404,8 @@
 
 
 def fluid_kernel(*refs):
-    patch, fields, table_hbm, disp, acc, work, table, table_sem, got = refs[:9]
-    names, data = refs[9 : 9 + SLOTS], refs[9 + SLOTS :]
+    patch, fields, table_hbm, disp, acc, work, table, held, table_sem, got = refs[:10]
+    names, data = refs[10 : 10 + SLOTS], refs[10 + SLOTS :]
     fill = pltpu.make_async_copy(table_hbm, table, table_sem)
     fill.start()
     points = disp.shape[1]
@@ -423,8 +423,6 @@
     for k in range(2):
         for copy in scalars(k):
             copy.start()
-    lane = lax.broadcasted_iota(jnp.int32, (8, LANES), 1)
-
     def patch_step(p, _):
         y = [table[6 * p + 2 * c] for c in range(3)]
         total = (y[0] * y[0] + y[1] * y[1]) + y[2] * y[2]
@@ -449,32 +447,24 @@
             for copy in scalars(1):
                 copy.wait()
 
-        def point_step(group, held):
-            first = group * 128
-            ahead = lane - first
-            held = list(held)
-            for q in range(128):
-                i = start + first + q
-                x, y, z, square = data[0][0, i], data[1][0, i], data[2][0, i], data[6][0, i]
-                ps = [names[s][0, i] for s in range(SLOTS)]
-                term = []
-                for s in range(SLOTS):
-                    p = ps[s] * 8
-                    near = (work[p] * x + work[p + 1] * y) + (work[p + 2] * z + (work[p + 3] + square))
-                    term.append(lax.rsqrt(near) * data[7 + s][0, i])
-                old = [[acc[p * 3 + c] for c in range(3)] for p in ps]
-                here = ahead == q
+        for q in range(LANES):
+            i = start + q
+            x, y, z, square = data[0][0, i], data[1][0, i], data[2][0, i], data[6][0, i]
+            ps = [names[s][0, i] for s in range(SLOTS)]
+            term = []
+            for s in range(SLOTS):
+                p = ps[s] * 8
+                near = (work[p] * x + work[p + 1] * y) + (work[p + 2] * z + (work[p + 3] + square))
+                term.append(lax.rsqrt(near) * data[7 + s][0, i])
+            old = [[acc[p * 3 + c] for c in range(3)] for p in ps]
+            for c in range(3):
+                dots = [work[ps[s] * 8 + 4 + c] * term[s] for s in range(SLOTS)]
+                value = (dots[0] + dots[1]) + (dots[2] + dots[3])
+                held[c, :, pl.ds(q, 1)] = jnp.sum(value, axis=1, keepdims=True)
+            force = [data[3 + c][0, i] for c in range(3)]
+            for s in range(SLOTS):
                 for c in range(3):
-                    dots = [work[ps[s] * 8 + 4 + c] * term[s] for s in range(SLOTS)]
-                    value = (dots[0] + dots[1]) + (dots[2] + dots[3])
-                    held[c] = jnp.where(here, jnp.sum(value, axis=1, keepdims=True), held[c])
-                force = [data[3 + c][0, i] for c in range(3)]
-                for s in range(SLOTS):
-                    for c in range(3):
-                        acc[ps[s] * 3 + c] = old[s][c] + term[s] * force[c]
-            return tuple(held)
-
-        held = lax.fori_loop(0, LANES // 128, point_step, (jnp.zeros((8, LANES), f32),) * 3)
+                    acc[ps[s] * 3 + c] = old[s][c] + term[s] * force[c]
         for c in range(3):
             total = jnp.sum(held[c], axis=0, keepdims=True)
             disp[pl.ds(c, 1), pl.ds(pl.multiple_of(start, LANES), LANES)] = total * (1.0 / 32.0)
@@ -496,6 +486,7 @@
         scratch_shapes=[
             VMEM((PATCHES * 8, 8, LANES), f32),
             VMEM((PATCHES * 6, 8, LANES), f32),
+            VMEM((3, 8, LANES), f32),
             pltpu.SemaphoreType.DMA,
             pltpu.SemaphoreType.DMA((2, SLOTS + FIELDS)),
         ]

time: 142 us -> 140 us (0.986)
  Pallas kernels: 139 us -> 137 us
    pallas_call x1, Pallas kernels: 62.1 us -> 59.8 us  [fluid(): pl.pallas_call(fluid_kernel, out_shape=(jax.ShapeDtypeStruct((3, points),...]
where the time goes in v6:
time: 140 us; the launch traced here: 139 us
  Pallas kernels  137 us (98%)
    pallas_call x1, Pallas kernels, fluid(): pl.pallas_call(fluid_kernel, out_shape=(jax.ShapeDtypeStruct((3, points),...  59.8 us
    pallas_call x1, Pallas kernels, patch_tables(): pl.pallas_call(patch_kernel, out_shape=(jax.ShapeDtypeStruct((4, 4, 4, 2,...  44.9 us
    pallas_call x1, Pallas kernels, node_sums(): pl.pallas_call(load_kernel, out_shape=jax.ShapeDtypeStruct((3, NODE_DEV),...  32 us

profile of v6, /device:TPU:0, one launch (start us, length us, event | category | flops | bytes accessed | tf_op | source)
XLA Modules:
  0.0 138.6 jit_solution(24977083332351471)
XLA Ops:
  0.6 44.9 %shard_map.95 = (f32[4,4,4,2,3,16,128]{6,5,4,3,2,1,0:T(8,128)}, f32[11,1,4096]{2,1,0:T(1,128)}, s32[4,1,4096]{2,1,0:T(1,128)}) custom-call(f32[3,512]{1,0:T(4,128)} %coords.1, f32[3,512]{1,0:T(4,128)} %disp.1, s32[1,1024]{1,0:T(1,128)} %ids.3, f32[1024,1024]{1,0:T(8,128)} %bitcast.5, f32[3,4096]{1,0:T(4,128)} %fluid_x.1, f32[3,4096]{1,0:T(4,128)} %fluid_f.1, ...), custom_call_target="tpu_custom_call" | custom-call | tf_op jit(solution)/shard_map/pallas_call | solution.py:321
  45.5 59.8 %shard_map.96 = (f32[3,4096]{1,0:T(4,128)}, f32[384,8,128]{2,1,0:T(8,128)}) custom-call(s32[4,1,4096]{2,1,0:T(1,128)} %get-tuple-element.7.refs_0_, f32[11,1,4096]{2,1,0:T(1,128)} %get-tuple-element.8.refs_1_, f32[768,8,128]{2,1,0:T(8,128)} %bitcast.7), custom_call_target="tpu_custom_call" | custom-call | tf_op jit(solution)/shard_map/pallas_call | solution.py:478
  105.4 32.0 %shard_map.97 = f32[3,512]{1,0:T(4,128)} custom-call(f32[4,4,4,2,3,8,128]{6,5,4,3,2,1,0:T(8,128)} %bitcast.8, s32[1,1024]{1,0:T(1,128)} %ids.3, f32[1024,1024]{1,0:T(8,128)} %bitcast.6), custom_call_target="tpu_custom_call" | custom-call | tf_op jit(solution)/shard_map/pallas_call | solution.py:384
  137.3 1.3 broadcast_multiply_fusion

commit v7 on v6

--- a/solution.py
+++ b/solution.py
@@ -127,7 +127,7 @@
         copy.wait()
 
 
-def sum_stages(terms, place_now, buffers, sems):
+def sum_stages(terms, place_now, buffers, sems, beside):
     me, core, spot = place_now
     core_in, s1, r2, s2, r3 = buffers
     plane_send, plane_recv, line_send, line_recv, core_send, core_recv = sems
@@ -151,6 +151,7 @@
                     peer_of(me, spot, g, step),
                 )
             )
+    beside()
     spread = [[], [], []]
     left = [[a for a in range(3) if a != g] for g in range(3)]
     for g in range(3):
@@ -347,11 +348,14 @@
     load.start()
     barrier = greet(me, core, spot, True)
     mark_local(ids, marks)
-    load.wait()
-    split_factor(factor, high, low)
     fill.wait()
     pl.semaphore_wait(barrier, PLANES)
-    summed = sum_stages(terms, (me, core, spot), patch_buffers, patch_sems)
+
+    def ready_factor():
+        load.wait()
+        split_factor(factor, high, low)
+
+    summed = sum_stages(terms, (me, core, spot), patch_buffers, patch_sems, ready_factor)
     rows = [jnp.concatenate([part[s : s + 1] for s in range(8)], axis=1) for part in summed]
     rows = jnp.concatenate(rows + [jnp.zeros((5, PN), f32)], axis=0)
     loads = apply_inverse(rows, high, low)
@@ -372,7 +376,7 @@
         for r in range(4):
             lanes = slice(r * LANES, (r + 1) * LANES)
             flat[pl.ds(4 * g + r, PATCHES, stride=12), :] = term[:, lanes]
-    owned = sum_stages(spread, (me, core, spot), node_buffers, node_sems)
+    owned = sum_stages(spread, (me, core, spot), node_buffers, node_sems, nothing)
     for g in range(3):
         for r in range(4):
             out[pl.ds(g, 1), pl.ds(r * LANES, LANES)] = owned[g][r : r + 1]

time: 140 us -> 139 us (level)
  no operation moved by 1% of the time
where the time goes in v7:
time: 139 us
  Pallas kernels  137 us (99%)
    pallas_call x1, Pallas kernels, fluid(): pl.pallas_call(fluid_kernel, out_shape=(jax.ShapeDtypeStruct((3, points),...  59.9 us
    pallas_call x1, Pallas kernels, patch_tables(): pl.pallas_call(patch_kernel, out_shape=(jax.ShapeDtypeStruct((4, 4, 4, 2,...  44.9 us
    pallas_call x1, Pallas kernels, node_sums(): pl.pallas_call(load_kernel, out_shape=jax.ShapeDtypeStruct((3, NODE_DEV),...  32 us

profile of v7, /device:TPU:0, one launch (start us, length us, event | category | flops | bytes accessed | tf_op | source)
XLA Modules:
  0.0 138.7 jit_solution(2128105885401450925)
XLA Ops:
  0.6 44.9 %shard_map.95 = (f32[4,4,4,2,3,16,128]{6,5,4,3,2,1,0:T(8,128)}, f32[11,1,4096]{2,1,0:T(1,128)}, s32[4,1,4096]{2,1,0:T(1,128)}) custom-call(f32[3,512]{1,0:T(4,128)} %coords.1, f32[3,512]{1,0:T(4,128)} %disp.1, s32[1,1024]{1,0:T(1,128)} %ids.3, f32[1024,1024]{1,0:T(8,128)} %bitcast.5, f32[3,4096]{1,0:T(4,128)} %fluid_x.1, f32[3,4096]{1,0:T(4,128)} %fluid_f.1, ...), custom_call_target="tpu_custom_call" | custom-call | tf_op jit(solution)/shard_map/pallas_call | solution.py:322
  45.5 59.9 %shard_map.96 = (f32[3,4096]{1,0:T(4,128)}, f32[384,8,128]{2,1,0:T(8,128)}) custom-call(s32[4,1,4096]{2,1,0:T(1,128)} %get-tuple-element.7.refs_0_, f32[11,1,4096]{2,1,0:T(1,128)} %get-tuple-element.8.refs_1_, f32[768,8,128]{2,1,0:T(8,128)} %bitcast.7), custom_call_target="tpu_custom_call" | custom-call | tf_op jit(solution)/shard_map/pallas_call | solution.py:482
  105.5 32.0 %shard_map.97 = f32[3,512]{1,0:T(4,128)} custom-call(f32[4,4,4,2,3,8,128]{6,5,4,3,2,1,0:T(8,128)} %bitcast.8, s32[1,1024]{1,0:T(1,128)} %ids.3, f32[1024,1024]{1,0:T(8,128)} %bitcast.6), custom_call_target="tpu_custom_call" | custom-call | tf_op jit(solution)/shard_map/pallas_call | solution.py:388
  137.4 1.3 broadcast_multiply_fusion
